TPU v7x, 256 devices: a whole 4x4x8 slice. The times are simulated.
256 devices in a mesh: req: 16 (over y, x), kv: 2 (over core), hid: 8 (over z).
Axes of the slice: x: 4, y: 4, z: 8, core: 2. Of those that a mesh axis runs over, the one named last changes fastest.
Arguments:
- tokens: bfloat16 [64, 8, 2048], P('req', 'hid'), may hold values from -6 to 6
- gains: float32 [4, 2048], replicated, may hold values from 0.1 to 1.9
- qk_gains: float32 [2, 256], replicated, may hold values from 0.1 to 1.9
- w_query: bfloat16 [2048, 2048], P('req', 'kv'), may hold values from -0.125 to 0.125
- key_value_weight: bfloat16 [2048, 2, 512], P('req', None, 'kv'), may hold values from -0.125 to 0.125
- output_weight: bfloat16 [2, 1024, 2048], P('kv', 'req'), may hold values from -0.125 to 0.125
- w_gateup: bfloat16 [2048, 2, 8192], P(None, None, ('kv', 'hid')), may hold values from -0.125 to 0.125
- w_down: bfloat16 [8192, 2048], P(('kv', 'hid')), may hold values from -0.0625 to 0.0625
- kv_cache: bfloat16 [5504, 2, 64, 512], P(('req', 'hid'), None, None, 'kv'), may hold values from -128 to 128
- lengths: int32 [64, 8], replicated, may hold values from 1 to 2048, as said below
- page_table: int32 [64, 8, 32], replicated, may hold values from -1 to 5503, as said below
Outputs:
- result: bfloat16 [64, 8, 2048], P(('req', 'kv'), 'hid')
Inputs may be any that keep to these rules, and one draw needn't show every extreme that they name: Request (j, g) belongs to tenant j % 4, whose lengths lie in max(1, c // 4) to c with c = 64, 128, 256 and 2048 for tenants 0 to 3. `page_table`: all pages of request (j, g) lie in one pool of its group: slots (r * 8 + g) * 43 to (r * 8 + g + 1) * 43 - 1 for one r; every pool holds the pages of 4 requests of its group, 1 of each tenant; entry p is -1 exactly where p * 64 >= lengths[j, g]; no slot is used twice.
All inputs are finite; a program needn't handle non-finite values.
Results may differ from a plain program's by a relative error of at most 0.035.
Values may be sent and summed in bfloat16 or wider, within the bound.
A program may use at most 64 MiB of HBM per device.

v0:
```python
import jax
import jax.numpy as jnp
from jax import lax
from jax.sharding import PartitionSpec as P

eps_norm = 1e-06
rope_base = 1000000.0
neg_large = -1e30


def combined_all(x, axis, combine):
    everything = jax.tree.map(
        lambda part, kind: lax.all_gather(part.astype(kind), axis),
        x,
        (jnp.bfloat16, jnp.bfloat16, jnp.bfloat16),
    )

    def take(k):
        return jax.tree.map(lambda part, own: part[k].astype(own.dtype), everything, x)

    return lax.fori_loop(
        1, lax.axis_size(axis), lambda k, so_far: combine(so_far, take(k)), take(0)
    )


def rms_scale(value_entries, gain_row):
    mean_square = jnp.mean(value_entries * value_entries, axis=-1, keepdims=True)
    return value_entries * lax.rsqrt(mean_square + eps_norm) * gain_row


def rotate(value_entries, position):
    half_width = value_entries.shape[-1] // 2
    frequency = rope_base ** (
        -jnp.arange(half_width, dtype=jnp.float32) * 2.0 / value_entries.shape[-1]
    )
    angles = position[:, None, None] * frequency
    cosines = jnp.cos(angles)
    sines = jnp.sin(angles)
    first_half = value_entries[..., :half_width]
    second_half = value_entries[..., half_width:]
    return jnp.concatenate(
        [first_half * cosines - second_half * sines, second_half * cosines + first_half * sines],
        axis=-1,
    )


def finish(summed, lengths_rows, qk_gains, per_group):
    head_width = qk_gains.shape[1]
    request_count = summed.shape[0]
    position = lengths_rows.astype(jnp.float32)
    split_at = per_group * head_width
    query = summed[:, :split_at].reshape(request_count, per_group, head_width)
    query = rotate(rms_scale(query, qk_gains[0]), position).astype(jnp.bfloat16)
    key_part = summed[:, split_at : split_at + head_width][:, None, :]
    key_new = rotate(rms_scale(key_part, qk_gains[1]), position)[:, 0].astype(jnp.bfloat16)
    value_new = rms_scale(summed[:, split_at + head_width :], 1.0).astype(jnp.bfloat16)
    return (query, key_new, value_new)


def attend_local(query, kv_cache, table_rows, group_lengths, slot_base):
    pool_size, _, page_size, head_width = kv_cache.shape
    request_count = table_rows.shape[0]
    local_slot = table_rows - slot_base
    usable = (local_slot >= 0) & (local_slot < pool_size)
    destination = jnp.where(usable, local_slot, pool_size).reshape(-1)
    requester = jnp.broadcast_to(
        jnp.arange(request_count, dtype=jnp.int32)[:, None], table_rows.shape
    ).reshape(-1)
    page_index = jnp.broadcast_to(
        jnp.arange(table_rows.shape[1], dtype=jnp.int32)[None, :], table_rows.shape
    ).reshape(-1)
    holder = jnp.full((pool_size,), -1, jnp.int32).at[destination].set(requester, mode="drop")
    page_number = jnp.zeros((pool_size,), jnp.int32).at[destination].set(page_index, mode="drop")
    clamped = jnp.maximum(holder, 0)
    query_slot = query[clamped]
    cached_keys = kv_cache[:, 0]
    cached_values = kv_cache[:, 1]
    scores = jnp.einsum(
        "phd,ptd->pht", query_slot, cached_keys, preferred_element_type=jnp.float32
    ) * head_width ** (-0.5)
    position = page_number[:, None] * page_size + jnp.arange(page_size, dtype=jnp.int32)[None, :]
    live_mask = ((holder[:, None] >= 0) & (position < group_lengths[clamped][:, None]))[:, None, :]
    masked = jnp.where(live_mask, scores, neg_large)
    slot_max = jnp.max(masked, axis=2)
    member_mask = holder[None, :] == jnp.arange(request_count, dtype=jnp.int32)[:, None]
    highest = jnp.max(jnp.where(member_mask[:, :, None], slot_max[None], neg_large), axis=1)
    weights = jnp.where(live_mask, jnp.exp(masked - highest[clamped][:, :, None]), 0.0)
    member_float = member_mask.astype(jnp.float32)
    totals = jnp.dot(member_float, jnp.sum(weights, axis=2), precision=lax.Precision.HIGHEST)
    mixed = jnp.einsum(
        "pht,ptd->phd",
        weights.astype(jnp.bfloat16),
        cached_values,
        preferred_element_type=jnp.float32,
    )
    weighted = jnp.dot(member_float, mixed.reshape(pool_size, -1), precision=lax.Precision.HIGHEST)
    return (highest, totals, weighted.reshape(request_count, -1, head_width))


def join_states(earlier, latter):
    highest = jnp.maximum(earlier[0], latter[0])
    scale_early = jnp.exp(earlier[0] - highest)
    scale_late = jnp.exp(latter[0] - highest)
    totals = earlier[1] * scale_early + latter[1] * scale_late
    weighted = earlier[2] * scale_early[..., None] + latter[2] * scale_late[..., None]
    return (highest, totals, weighted)


def finish_attention(highest_cached, totals, weighted, query, key_new, value_new):
    head_width = query.shape[-1]
    own_score = jnp.sum(
        query.astype(jnp.float32) * key_new.astype(jnp.float32)[:, None, :], axis=-1
    ) * head_width ** (-0.5)
    highest = jnp.maximum(highest_cached, own_score)
    old_scale = jnp.exp(highest_cached - highest)
    new_scale = jnp.exp(own_score - highest)
    combined = (
        weighted * old_scale[..., None]
        + new_scale[..., None] * value_new.astype(jnp.float32)[:, None, :]
    ) / (totals * old_scale + new_scale)[..., None]
    return combined.astype(jnp.bfloat16)


def shards(
    tokens,
    gains,
    qk_gains,
    w_query,
    key_value_weight,
    output_weight,
    w_gateup,
    w_down,
    kv_cache,
    lengths,
    page_table,
):
    req_position = lax.axis_index("req")
    kv_position = lax.axis_index("kv")
    hid_position = lax.axis_index("hid")
    hid_total = lax.axis_size("hid")
    rows_here = tokens.shape[0]
    half_rows = rows_here // lax.axis_size("kv")
    own_rows = tokens[:, 0, :].astype(jnp.float32)
    normed = rms_scale(own_rows, gains[0]).astype(jnp.bfloat16)
    columns = lax.all_to_all(normed, "req", split_axis=1, concat_axis=0, tiled=True)
    request_count = columns.shape[0]
    head_width = qk_gains.shape[1]
    per_group = w_query.shape[1] // head_width
    projection = jnp.concatenate(
        [w_query, key_value_weight.reshape(key_value_weight.shape[0], -1)], axis=1
    )
    group_lengths = lax.dynamic_index_in_dim(lengths, hid_position, axis=1, keepdims=False)
    group_table = lax.dynamic_index_in_dim(page_table, hid_position, axis=1, keepdims=False)
    partial_all = jnp.dot(columns, projection, preferred_element_type=jnp.float32)
    summed = lax.psum(partial_all, "req")
    query, key_new, value_new = finish(summed, group_lengths, qk_gains, per_group)
    pool_size = kv_cache.shape[0]
    slot_base = (req_position * hid_total + hid_position) * pool_size
    local_highest, local_totals, local_weighted = attend_local(
        query, kv_cache, group_table, group_lengths, slot_base
    )
    slice_width = output_weight.shape[1]
    highest, totals, weighted = combined_all(
        (local_highest, local_totals, local_weighted), "req", join_states
    )
    attended = finish_attention(highest, totals, weighted, query, key_new, value_new).reshape(
        request_count, -1
    )
    head_dims = lax.dynamic_slice_in_dim(attended, req_position * slice_width, slice_width, 1)
    projected = lax.psum_scatter(
        jnp.dot(head_dims, output_weight[0], preferred_element_type=jnp.float32).astype(
            jnp.bfloat16
        ),
        ("req", "kv"),
        scatter_dimension=0,
        tiled=True,
    ).astype(jnp.float32)
    residual = lax.dynamic_slice_in_dim(own_rows, kv_position * half_rows, half_rows, 0)
    middle = (residual + rms_scale(projected, gains[1])).astype(jnp.bfloat16)
    ffn_input = rms_scale(middle.astype(jnp.float32), gains[2]).astype(jnp.bfloat16)
    gate_up = jnp.einsum(
        "nd,dgf->ngf",
        lax.all_gather(ffn_input, ("kv", "hid"), axis=0, tiled=True),
        w_gateup,
        preferred_element_type=jnp.float32,
    )
    hidden = (jax.nn.gelu(gate_up[:, 0], approximate=True) * gate_up[:, 1]).astype(jnp.bfloat16)
    ffn_sum = lax.psum_scatter(
        jnp.dot(hidden, w_down, preferred_element_type=jnp.float32).astype(jnp.bfloat16),
        ("kv", "hid"),
        scatter_dimension=0,
        tiled=True,
    ).astype(jnp.float32)
    result = (middle.astype(jnp.float32) + rms_scale(ffn_sum, gains[3])).astype(jnp.bfloat16)
    return result[:, None, :]


def solution(mesh):
    return jax.shard_map(
        shards,
        mesh=mesh,
        in_specs=(
            P("req", "hid", None),
            P(),
            P(),
            P("req", "kv"),
            P("req", None, "kv"),
            P("kv", "req", None),
            P(None, None, ("kv", "hid")),
            P(("kv", "hid"), None),
            P(("req", "hid"), None, None, "kv"),
            P(),
            P(),
        ),
        out_specs=P(("req", "kv"), "hid", None),
        check_vma=False,
    )
```

profile of v0, /device:TPU:1, one launch (start us, length us, event | category | flops | bytes accessed | tf_op | source)
XLA Modules:
  0.0 481.4 jit_solution(10238840653166389767)
XLA Ops:
  6.5 1.0 fusion.97
  7.5 0.8 multiply_reduce_fusion.4
  8.4 1.4 fusion.51
  9.8 7.6 %all-to-all-start = ((bf16[4,16,128]{2,0,1:T(4,128)(2,1)}), bf16[4,16,128]{2,0,1:T(4,128)(2,1)S(1)}, u32[]{:S(2)}, u32[]{:S(2)}) async-start(bf16[4,16,128]{2,0,1:T(4,128)(2,1)} %fusion.51), calls=%async_computation | async-start | bytes 32768 | tf_op jit(solution)/shard_map/all_to_all | solution.py:145
  17.5 0.7 dynamic-slice_subtract_fusion
  18.5 8.0 %scatter_custom_fusion = s32[43]{0:T(128)S(1)} fusion(s32[2048]{0:T(1024)S(1)} %bitcast.129, s32[2048]{0:T(1024)S(1)} %reshape.401, s32[]{:T(128)} %constant.107.clone.1), kind=kCustom, calls=%fused_computation.149 | custom fusion | bytes 176 | tf_op jit(solution)/shard_map/scatter | solution.py:72
  26.5 0.7 fusion.95
  27.3 8.0 %scatter_custom_fusion.1 = s32[43]{0:T(128)S(1)} fusion(s32[2048]{0:T(1024)S(1)} %bitcast.130, s32[2048]{0:T(1024)S(1)} %reshape.409, s32[]{:T(128)} %constant.105.clone.1), kind=kCustom, calls=%fused_computation.146 | custom fusion | bytes 176 | tf_op jit(solution)/shard_map/scatter | solution.py:73
  35.4 0.8 gather_fusion
  36.3 0.9 copy.106
  37.3 1.9 fusion.18
  39.5 96.4 %all-reduce.6.cloned.1.call-done = f32[64,1536]{1,0:T(8,128)} async-done(((f32[64,1536]{1,0:T(8,128)}), f32[64,1536]{1,0:T(8,128)}) %all-reduce.6.cloned.1.call-update) | async-done | bytes 393232 | tf_op jit(solution)/shard_map/psum | solution.py:155
  135.8 1.0 slice.91
  137.4 0.6 gather_fusion.1
  138.1 1.9 fusion.99
  140.8 1.7 fusion.5
  142.7 1.0 convolution_convert_fusion.2
  144.9 16.4 %all-gather.4 = bf16[16,64,4]{1,2,0:T(4,128)(2,1)S(1)} all-gather(bf16[1,64,4]{1,2,0:T(4,128)(2,1)S(1)} %fusion.17), channel_id=3, replica_groups=mesh['req'=16,'kv'=2,'hid'=8] {'req'}, dimensions={0}, use_global_device_ids=true | all-gather | bytes 8704 | tf_op jit(solution)/shard_map/all_gather | solution.py:13
  161.4 16.5 %all-gather.3 = bf16[16,64,4]{1,2,0:T(4,128)(2,1)S(1)} all-gather(bf16[1,64,4]{1,2,0:T(4,128)(2,1)S(1)} %convert_bitcast_fusion), channel_id=2, replica_groups=mesh['req'=16,'kv'=2,'hid'=8] {'req'}, dimensions={0}, use_global_device_ids=true | all-gather | bytes 8704 | tf_op jit(solution)/shard_map/all_gather | solution.py:13
  177.8 15.9 %all-gather.8.cloned.1.call-done = bf16[1024,4,256]{2,0,1:T(8,128)(2,1)} async-done(((bf16[64,4,256]{2,0,1:T(8,128)(2,1)}), bf16[1024,4,256]{2,0,1:T(8,128)(2,1)}) %all-gather.8.cloned.1.call-update) | async-done | bytes 2097168 | tf_op jit(solution)/shard_map/all_gather | solution.py:13
  193.8 0.9 slice_convert_fusion
  194.9 23.8 %while.19 = (s32[]{:T(128)}, f32[64,4]{0,1:T(4,128)S(1)}, f32[64,4]{0,1:T(4,128)S(1)}, f32[64,4,256]{2,1,0:T(4,128)S(1)}, bf16[16,64,4]{1,2,0:T(4,128)(2,1)S(1)}...) while((s32[]{:T(128)}, f32[64,4]{0,1:T(4,128)S(1)}, ...), condition=%wide.region_9.10_spmd, body=%wide.region_8.9_spmd.sunk | while | flops 264197 | bytes 930967 | solution.py:21
  195.1 0.9 constant_dynamic-slice_fusion.4
  196.7 0.9 constant_dynamic-slice_fusion.4
  198.3 0.9 constant_dynamic-slice_fusion.4
  199.9 0.9 constant_dynamic-slice_fusion.4
  201.5 0.9 constant_dynamic-slice_fusion.4
  203.1 0.9 constant_dynamic-slice_fusion.4
  204.6 0.9 constant_dynamic-slice_fusion.4
  206.2 0.9 constant_dynamic-slice_fusion.4
  207.8 0.9 constant_dynamic-slice_fusion.4
  209.4 0.9 constant_dynamic-slice_fusion.4
  211.0 0.9 constant_dynamic-slice_fusion.4
  212.6 0.9 constant_dynamic-slice_fusion.4
  214.2 0.9 constant_dynamic-slice_fusion.4
  215.7 0.9 constant_dynamic-slice_fusion.4
  217.3 0.9 constant_dynamic-slice_fusion.4
  219.3 1.0 convolution_convert_fusion
  221.6 110.4 %all-reduce.8.cloned.1.call-done = bf16[64,2048]{1,0:T(8,128)(2,1)} async-done(((bf16[64,2048]{1,0:T(8,128)(2,1)}), bf16[64,2048]{1,0:T(8,128)(2,1)}) %all-reduce.8.cloned.1.call-update) | async-done | bytes 262160
  332.0 0.9 fusion.58
  332.9 1.0 fusion.64
  334.0 28.3 %all-gather.5 = bf16[16,2,2048]{2,1,0:T(2,128)(2,1)S(1)} all-gather(bf16[1,2,2048]{2,1,0:T(2,128)(2,1)S(1)} %fusion.73), channel_id=1, replica_groups=mesh['req'=16,'kv'=2,'hid'=8] {'kv','hid'}, dimensions={0}, use_global_device_ids=true | all-gather | bytes 139264 | tf_op jit(solution)/shard_map/all_gather | solution.py:183
  362.4 3.0 fusion.3
  365.4 1.1 convolution_convert_fusion.1
  366.6 0.6 dynamic-slice.3
  367.8 104.7 %all-reduce.10.cloned.1.call-done = bf16[32,2048]{1,0:T(8,128)(2,1)} async-done(((bf16[32,2048]{1,0:T(8,128)(2,1)}), bf16[32,2048]{1,0:T(8,128)(2,1)}) %all-reduce.10.cloned.1.call-update) | async-done | bytes 131088
  472.5 0.9 fusion.62
  473.4 1.4 fusion.74
  (138 shorter events, 14.9 us)
Async XLA Ops:
  6.5 358.9 %copy-start = (bf16[512,2048]{1,0:T(8,128)(2,1)S(1)}, bf16[512,2048]{1,0:T(8,128)(2,1)}, u32[]{:S(2)}) copy-start(bf16[512,2048]{1,0:T(8,128)(2,1)} %param.20) | copy-start | bytes 6291460
  6.5 32.7 %copy-start.4 = (f32[2,256]{1,0:T(2,128)S(1)}, f32[2,256]{1,0:T(2,128)}, u32[]{:S(2)}) copy-start(f32[2,256]{1,0:T(2,128)} %param.15) | copy-start | bytes 6148
  9.8 27.4 %all-to-all-start = ((bf16[4,16,128]{2,0,1:T(4,128)(2,1)}), bf16[4,16,128]{2,0,1:T(4,128)(2,1)S(1)}, u32[]{:S(2)}, u32[]{:S(2)}) async-start(bf16[4,16,128]{2,0,1:T(4,128)(2,1)} %fusion.51), calls=%async_computation | async-start | bytes 32768 | tf_op jit(solution)/shard_map/all_to_all | solution.py:145
  17.4 118.4 %all-reduce.6.cloned.1.call-start = ((), (), s32[]{:S(2)}) async-start(), calls=%async_computation.1 | async-start | bytes 786432 | tf_op jit(solution)/shard_map/psum | solution.py:155
  39.2 154.6 %all-gather.8.cloned.1.call-start = ((), (), s32[]{:S(2)}) async-start(), calls=%async_computation.2 | async-start | bytes 2228224 | tf_op jit(solution)/shard_map/all_gather | solution.py:13
  140.0 3.8 copy-start.1
  143.8 188.3 %all-reduce.8.cloned.1.call-start = ((), (), s32[]{:S(2)}) async-start(), calls=%async_computation.3 | async-start | bytes 524288
  194.9 24.4 %copy-start.2 = (bf16[1,64,2048]{2,1,0:T(8,128)(2,1)S(1)}, bf16[1,64,2048]{2,1,0:T(8,128)(2,1)}, u32[]{:S(2)}) copy-start(bf16[1,64,2048]{2,1,0:T(8,128)(2,1)} %param.18) | copy-start | bytes 786436
  194.9 25.5 %copy-start.3 = (bf16[4,1,2048]{2,0,1:T(4,128)(2,1)S(1)}, bf16[4,1,2048]{2,0,1:T(4,128)(2,1)}, u32[]{:S(2)}) copy-start(bf16[4,1,2048]{2,0,1:T(4,128)(2,1)} %param.13) | copy-start | bytes 49156
  194.9 25.5 %copy-start.6 = (u32[256]{0:T(256)S(1)}, u32[256]{0:T(256)}, u32[]{:S(2)}) copy-start(u32[256]{0:T(256)} %constant.133) | copy-start | bytes 3076
  220.3 252.2 %all-reduce.10.cloned.1.call-start = ((), (), s32[]{:S(2)}) async-start(), calls=%async_computation.4 | async-start | bytes 262144
  365.4 1.1 copy-start.5
Sparse Core Ops, SparseCore 0:
  39.3 96.5 all-reduce.5
  143.9 49.8 all-gather.7
  220.4 111.5 all-reduce.7
  366.7 105.7 all-reduce.9
where the time goes:
time: 482 us; the launch traced here: 481 us
  waiting for transfers between devices  327 us (68%)
  blocking collectives  61.2 us (13%)
  local copies, waits for them, and re-layouts  40.1 us (8%)
  other arithmetic  17.8 us (4%)
  between operations  14.8 us (3%)
  matrix products  11.9 us (2%)
  starting transfers between devices  7.75 us (2%)
    unnamed x6, waiting for transfers between devices  215 us
    psum x1, waiting for transfers between devices, shards(): summed = lax.psum(partial_all, 'req')  96.4 us
    all_gather x2, blocking collectives, combined_all(): lax.all_gather(part.astype(kind), axis)  32.9 us
    all_gather x1, blocking collectives, shards(): lax.all_gather(ffn_input, ('kv', 'hid'), axis=0, tiled=True)  28.3 us
    all_gather x1, waiting for transfers between devices, combined_all(): lax.all_gather(part.astype(kind), axis)  15.9 us
    dynamic_slice x15, local copies, waits for them, and re-layouts, take(): part[k].astype(own.dtype)  13.7 us
  transfers between devices with their start and end apart: 5, of which 4 were waited for; matrix products, arithmetic and copies ran while one was open for 5% of the time, Pallas kernels for 0%

commit v1 on v0

v1 whole, which is shorter than its diff:
```python
import functools

import jax
import jax.numpy as jnp
from jax import lax
from jax.experimental import pallas as pl
from jax.experimental.pallas import tpu as pltpu
from jax.sharding import PartitionSpec as P

eps_norm = 1e-06
rope_base = 1000000.0
neg_large = -1e30
MESH = pl.DeviceIdType.MESH
AXES = ("req", "kv", "hid")


def group_layout(group):
    sizes = [lax.axis_size(a) for a in group]
    me = 0
    for a, s in zip(group, sizes):
        me = me * s + lax.axis_index(a)
    total = 1
    for s in sizes:
        total *= s
    return sizes, me, total


def device_of(group, sizes, position):
    coords = {a: lax.axis_index(a) for a in AXES}
    rest = position
    for a, s in reversed(list(zip(group, sizes))):
        coords[a] = rest % s
        rest = rest // s
    return tuple(coords[a] for a in AXES)


def exchange_kernel(group, bcast, x_ref, y_ref, send_sem, recv_sem):
    sizes, me, n = group_layout(group)
    barrier = pltpu.get_barrier_semaphore()
    for s in range(1, n):
        peer = lax.rem(me + s, n)
        pl.semaphore_signal(
            barrier, inc=1, device_id=device_of(group, sizes, peer), device_id_type=MESH
        )
    pl.semaphore_wait(barrier, n - 1)
    copies = []
    for s in range(1, n):
        peer = lax.rem(me + s, n)
        src = x_ref if bcast else x_ref.at[peer]
        copy = pltpu.make_async_remote_copy(
            src_ref=src,
            dst_ref=y_ref.at[me],
            send_sem=send_sem.at[s],
            recv_sem=recv_sem.at[s],
            device_id=device_of(group, sizes, peer),
            device_id_type=MESH,
        )
        copy.start()
        copies.append(copy)
    if bcast:
        y_ref[me] = x_ref[...]
    else:
        y_ref[me] = x_ref[me]
    for s in range(1, n):
        copies[s - 1].wait_send()
        origin = lax.rem(me + n - s, n)
        src = x_ref if bcast else x_ref.at[origin]
        pltpu.make_async_remote_copy(
            src_ref=src,
            dst_ref=y_ref.at[origin],
            send_sem=send_sem.at[s],
            recv_sem=recv_sem.at[s],
            device_id=device_of(group, sizes, origin),
            device_id_type=MESH,
        ).wait_recv()


def exchange(x, group, cid, bcast=False):
    n = 1
    for a in group:
        n *= lax.axis_size(a)
    block = x.shape if bcast else x.shape[1:]
    return pl.pallas_call(
        functools.partial(exchange_kernel, group, bcast),
        out_shape=jax.ShapeDtypeStruct((n,) + tuple(block), x.dtype),
        in_specs=[pl.BlockSpec(memory_space=pltpu.VMEM)],
        out_specs=pl.BlockSpec(memory_space=pltpu.VMEM),
        scratch_shapes=[pltpu.SemaphoreType.DMA((n,)), pltpu.SemaphoreType.DMA((n,))],
        compiler_params=pltpu.CompilerParams(collective_id=cid, has_side_effects=True),
    )(x)


def rms_scale(value_entries, gain_row):
    mean_square = jnp.mean(value_entries * value_entries, axis=-1, keepdims=True)
    return value_entries * lax.rsqrt(mean_square + eps_norm) * gain_row


def rotate(value_entries, position):
    half_width = value_entries.shape[-1] // 2
    frequency = rope_base ** (
        -jnp.arange(half_width, dtype=jnp.float32) * 2.0 / value_entries.shape[-1]
    )
    angles = position[:, None, None] * frequency
    cosines = jnp.cos(angles)
    sines = jnp.sin(angles)
    first_half = value_entries[..., :half_width]
    second_half = value_entries[..., half_width:]
    return jnp.concatenate(
        [first_half * cosines - second_half * sines, second_half * cosines + first_half * sines],
        axis=-1,
    )


def shards(
    tokens,
    gains,
    qk_gains,
    w_query,
    key_value_weight,
    output_weight,
    w_gateup,
    w_down,
    kv_cache,
    lengths,
    page_table,
):
    req_position = lax.axis_index("req")
    kv_position = lax.axis_index("kv")
    hid_position = lax.axis_index("hid")
    req_total = lax.axis_size("req")
    hid_total = lax.axis_size("hid")
    kv_total = lax.axis_size("kv")
    rows_here, _, model_width = tokens.shape
    half_rows = rows_here // kv_total
    head_width = qk_gains.shape[1]
    per_group = w_query.shape[1] // head_width
    pool_size, _, page_size, _ = kv_cache.shape
    request_count = rows_here * req_total
    feature_width = w_query.shape[0]

    own_rows = tokens[:, 0, :].astype(jnp.float32)
    normed = rms_scale(own_rows, gains[0]).astype(jnp.bfloat16)

    send_tokens = normed.reshape(rows_here, req_total, feature_width).transpose(1, 0, 2)
    columns = exchange(send_tokens, ("req",), 0).reshape(request_count, feature_width)

    group_lengths = lax.dynamic_index_in_dim(lengths, hid_position, axis=1, keepdims=False)
    group_table = lax.dynamic_index_in_dim(page_table, hid_position, axis=1, keepdims=False)
    request_ids = jnp.arange(request_count, dtype=jnp.int32)
    pool_of = (group_table[:, 0] // pool_size) // hid_total
    pool_pos = pool_of * rows_here + request_ids % rows_here
    order = pool_pos[None, :] == request_ids[:, None]
    order_b = order.astype(jnp.bfloat16)
    columns_pooled = jnp.dot(order_b, columns, preferred_element_type=jnp.float32).astype(
        jnp.bfloat16
    )

    projection = jnp.concatenate(
        [w_query, key_value_weight.reshape(key_value_weight.shape[0], -1)], axis=1
    )
    partial = jnp.dot(columns_pooled, projection, preferred_element_type=jnp.float32)
    gathered = exchange(partial.reshape(req_total, rows_here, -1), ("req",), 1)
    summed = jnp.sum(gathered, axis=0)

    mine = lax.dynamic_slice_in_dim(order, req_position * rows_here, rows_here, 0)
    my_lengths = jnp.sum(jnp.where(mine, group_lengths[None, :], 0), axis=1)
    my_tables = jnp.sum(jnp.where(mine[:, :, None], group_table[None, :, :], 0), axis=1)

    position = my_lengths.astype(jnp.float32)
    split_at = per_group * head_width
    query = summed[:, :split_at].reshape(rows_here, per_group, head_width)
    query = rotate(rms_scale(query, qk_gains[0]), position).astype(jnp.bfloat16)
    key_part = summed[:, split_at : split_at + head_width][:, None, :]
    key_new = rotate(rms_scale(key_part, qk_gains[1]), position)[:, 0].astype(jnp.bfloat16)
    value_new = rms_scale(summed[:, split_at + head_width :], 1.0).astype(jnp.bfloat16)

    slot_base = (req_position * hid_total + hid_position) * pool_size
    local = my_tables - slot_base
    slots = jnp.arange(pool_size, dtype=jnp.int32)
    match = local[:, :, None] == slots[None, None, :]
    page_ids = jnp.arange(my_tables.shape[1], dtype=jnp.int32)
    owner_hit = jnp.any(match, axis=1)
    page_of = jnp.sum(jnp.where(match, page_ids[None, :, None], 0), axis=(0, 1))
    cache_pos = page_of[:, None] * page_size + jnp.arange(page_size, dtype=jnp.int32)[None, :]
    live = owner_hit[:, :, None] & (cache_pos[None] < my_lengths[:, None, None])
    live = live.reshape(rows_here, 1, pool_size * page_size)

    cached_keys = kv_cache[:, 0].reshape(pool_size * page_size, head_width)
    cached_values = kv_cache[:, 1].reshape(pool_size * page_size, head_width)
    scale_factor = head_width ** (-0.5)
    scores = jnp.dot(
        query.reshape(rows_here * per_group, head_width),
        cached_keys.T,
        preferred_element_type=jnp.float32,
    ).reshape(rows_here, per_group, -1) * scale_factor
    masked = jnp.where(live, scores, neg_large)
    highest_cached = jnp.max(masked, axis=2)
    weights = jnp.where(live, jnp.exp(masked - highest_cached[..., None]), 0.0)
    totals = jnp.sum(weights, axis=2)
    weighted = jnp.dot(
        weights.astype(jnp.bfloat16).reshape(rows_here * per_group, -1),
        cached_values,
        preferred_element_type=jnp.float32,
    ).reshape(rows_here, per_group, head_width)
    query_f = query.astype(jnp.float32)
    own_score = jnp.sum(query_f * key_new.astype(jnp.float32)[:, None, :], axis=-1) * scale_factor
    highest = jnp.maximum(highest_cached, own_score)
    old_scale = jnp.exp(highest_cached - highest)
    new_scale = jnp.exp(own_score - highest)
    combined = (
        weighted * old_scale[..., None]
        + new_scale[..., None] * value_new.astype(jnp.float32)[:, None, :]
    ) / (totals * old_scale + new_scale)[..., None]
    attended = combined.astype(jnp.bfloat16).reshape(rows_here, per_group * head_width)

    slice_width = output_weight.shape[1]
    send_att = attended.reshape(rows_here, req_total, slice_width).transpose(1, 0, 2)
    got_att = exchange(send_att, ("req",), 2).reshape(request_count, slice_width)
    att_natural = jnp.dot(order_b.T, got_att, preferred_element_type=jnp.float32).astype(
        jnp.bfloat16
    )
    proj_partial = jnp.dot(att_natural, output_weight[0], preferred_element_type=jnp.float32)
    proj_partial = proj_partial.astype(jnp.bfloat16).reshape(
        req_total * kv_total, half_rows, model_width
    )
    projected = jnp.sum(
        exchange(proj_partial, ("req", "kv"), 3).astype(jnp.float32), axis=0
    )

    residual = lax.dynamic_slice_in_dim(own_rows, kv_position * half_rows, half_rows, 0)
    middle = (residual + rms_scale(projected, gains[1])).astype(jnp.bfloat16)
    ffn_input = rms_scale(middle.astype(jnp.float32), gains[2]).astype(jnp.bfloat16)
    ffn_rows = exchange(ffn_input, ("kv", "hid"), 4, bcast=True).reshape(-1, model_width)
    gate_up = jnp.einsum(
        "nd,dgf->ngf", ffn_rows, w_gateup, preferred_element_type=jnp.float32
    )
    hidden = (jax.nn.gelu(gate_up[:, 0], approximate=True) * gate_up[:, 1]).astype(jnp.bfloat16)
    ffn_partial = jnp.dot(hidden, w_down, preferred_element_type=jnp.float32).astype(
        jnp.bfloat16
    )
    ffn_partial = ffn_partial.reshape(kv_total * hid_total, half_rows, model_width)
    ffn_sum = jnp.sum(exchange(ffn_partial, ("kv", "hid"), 5).astype(jnp.float32), axis=0)
    result = (middle.astype(jnp.float32) + rms_scale(ffn_sum, gains[3])).astype(jnp.bfloat16)
    return result[:, None, :]


def solution(mesh):
    return jax.shard_map(
        shards,
        mesh=mesh,
        in_specs=(
            P("req", "hid", None),
            P(),
            P(),
            P("req", "kv"),
            P("req", None, "kv"),
            P("kv", "req", None),
            P(None, None, ("kv", "hid")),
            P(("kv", "hid"), None),
            P(("req", "hid"), None, None, "kv"),
            P(),
            P(),
        ),
        out_specs=P(("req", "kv"), "hid", None),
        check_vma=False,
    )
```

time: 482 us -> 94.7 us (0.20)
  waiting for transfers between devices: 327 us -> 0 us
  Pallas kernels: 0 us -> 67.7 us
  blocking collectives: 61.2 us -> 0 us
  local copies, waits for them, and re-layouts: 40.1 us -> 10.1 us
  between operations: 14.8 us -> 0.24 us
  other arithmetic: 17.8 us -> 9.01 us
  starting transfers between devices: 7.75 us -> 0 us
  matrix products: 11.9 us -> 6.84 us
    unnamed x6 -> x0, waiting for transfers between devices: 215 us -> none
    psum x1 -> x0, waiting for transfers between devices: 96.4 us -> none  [shards(): summed = lax.psum(partial_all, 'req')]
    pallas_call x0 -> x6, Pallas kernels: none -> 67.7 us  [exchange(): pl.pallas_call(functools.partial(exchange_kernel, group, bcast), out_shap...]
    all_gather x3 -> x0, blocking collectives: 61.2 us -> none  [the longest x2 32.9 us: combined_all(): lax.all_gather(part.astype(kind), axis)]
    scatter x2 -> x0, local copies, waits for them, and re-layouts: 16.1 us -> none  [the longest x1 8.03 us: attend_local(): jnp.full((pool_size,), -1, jnp.int32).at[destination]]
    all_gather x1 -> x0, waiting for transfers between devices: 15.9 us -> none  [combined_all(): lax.all_gather(part.astype(kind), axis)]
    dynamic_slice x15 -> x0, local copies, waits for them, and re-layouts: 13.7 us -> none  [take(): part[k].astype(own.dtype)]
    all_to_all x1 -> x0, starting transfers between devices: 7.58 us -> none  [shards(): lax.all_to_all(normed, 'req', split_axis=1, concat_axis=0, tiled=True)]
  transfers between devices with their start and end apart: 5 -> 0, of which waited for: 4 -> 0; matrix products, arithmetic and copies ran while one was open for 5% -> 0% of each run, Pallas kernels for 0% -> 0%
where the time goes in v1:
time: 94.7 us; the launch traced here: 93.9 us
  Pallas kernels  67.7 us (71%)
  local copies, waits for them, and re-layouts  10.1 us (11%)
  other arithmetic  9.01 us (10%)
  matrix products  6.84 us (7%)
    pallas_call x6, Pallas kernels, exchange(): pl.pallas_call(functools.partial(exchange_kernel, group, bcast), out_shap...  67.7 us
    dot_general x1, matrix products, shards(): jnp.einsum('nd,dgf->ngf', ffn_rows, w_gateup, preferred_element_type=jnp....  3.01 us
    slice x1, local copies, waits for them, and re-layouts, shards(): cached_keys = kv_cache[:, 0].reshape(pool_size * page_size, head_width)  1.98 us

profile of v1, /device:TPU:1, one launch (start us, length us, event | category | flops | bytes accessed | tf_op | source)
XLA Modules:
  0.0 93.9 jit_solution(1117368645274015472)
XLA Ops:
  0.0 0.9 dynamic-slice_bitcast_fusion
  0.9 0.9 %fusion.71 = (f32[1,2048]{1,0:T(1,128)S(1)}, f32[1,2048]{1,0:T(1,128)S(1)}, f32[1,2048]{1,0:T(1,128)S(1)}, f32[1,2048]{1,0:T(1,128)S(1)}) fusion(f32[4,2048]{1,0:T(4,128)} %param.12), kind=kLoop, calls=%fused_computation.129 | loop fusion | bytes 65536 | tf_op jit(solution)/shard_map/slice | solution.py:232
  1.9 0.8 multiply_reduce_fusion
  2.7 1.4 %fusion.38.x_ref = bf16[16,4,128]{2,1,0:T(4,128)(2,1)} fusion(f32[16,128]{1,0:T(8,128)S(1)} %bitcast.83, f32[4]{0:T(128)S(1)} %add_rsqrt_fusion.6, bf16[4,1,2048]{2,0,1:T(4,128)(2,1)} %param.11), kind=kLoop, calls=%fused_computation.58 | loop fusion | flops 32768 | bytes 40976 | tf_op jit(solution)/shard_map/transpose | solution.py:144
  4.1 10.5 %shard_map.109 = bf16[16,4,128]{2,1,0:T(4,128)(2,1)} custom-call(bf16[16,4,128]{2,1,0:T(4,128)(2,1)} %fusion.38.x_ref), custom_call_target="tpu_custom_call" | custom-call | tf_op jit(solution)/shard_map/pallas_call | solution.py:83
  14.6 0.9 copy.19
  15.5 1.3 %fusion.5 = f32[64,1536]{1,0:T(8,128)S(1)} fusion(bf16[64,128]{1,0:T(8,128)(2,1)} %bitcast.77, bf16[128,512]{1,0:T(8,128)(2,1)S(1)} %bitcast.75, bf16[128,1024]{1,0:T(8,128)(2,1)} %param.14, s32[64]{0:T(128)S(1)} %fusion.58), kind=kOutput, calls=%fused_computation.11 | convolution fusion | flops 27013120 | bytes 803072 | tf_op jit(solution)/shard_map/dot_general | solution.py:161
  16.8 0.8 reshape.382.x_ref
  17.6 9.9 %shard_map.110 = f32[16,4,1536]{2,1,0:T(4,128)} custom-call(f32[16,4,1536]{2,1,0:T(4,128)} %reshape.382.x_ref), custom_call_target="tpu_custom_call" | custom-call | tf_op jit(solution)/shard_map/pallas_call | solution.py:83
  27.5 1.1 %reduce_sum.139 = f32[4,1536]{1,0:T(4,128)S(1)} reduce(f32[16,4,1536]{2,1,0:T(4,128)} %shard_map.110, f32[]{:T(128)} %constant.99.clone.1), dimensions={0}, to_apply=%region_5.6 | reduce | flops 92160 | bytes 417796 | tf_op jit(solution)/shard_map/reduce_sum | solution.py:163
  28.6 0.1 multiply_reduce_fusion.5
  28.9 0.7 fusion.59
  29.6 0.1 select_reduce_fusion.2
  29.7 0.1 fusion.57
  29.8 0.1 multiply_cosine_fusion.1
  30.0 0.1 multiply_reduce_fusion.4
  30.1 0.1 multiply_multiply_fusion.1
  30.2 0.1 multiply_reduce_fusion.3
  30.3 0.1 select_reduce_fusion.1
  30.4 0.1 select_reduce_fusion
  30.5 0.1 broadcast_reduce_fusion
  30.8 0.1 fusion.26
  30.9 0.1 and.56
  31.1 0.1 and.57
  31.2 0.1 compare_and_fusion
  31.2 2.0 %fusion.70 = (bf16[43,1,64,256]{3,2,1,0:T(8,128)(2,1)S(1)}, bf16[43,1,64,256]{3,2,1,0:T(8,128)(2,1)S(1)}) fusion(bf16[43,2,64,256]{3,2,1,0:T(8,128)(2,1)} %param.19), kind=kLoop, calls=%fused_computation.128 | loop fusion | bytes 5636096 | tf_op jit(solution)/shard_map/slice | solution.py:188
  33.2 0.6 fusion.73
  33.8 0.2 fusion.11
  34.1 0.4 fusion.6
  34.5 0.1 reshape_reshape.3
  34.6 0.6 copy.23
  35.2 8.7 %shard_map.111 = bf16[16,4,64]{2,1,0:T(4,128)(2,1)} custom-call(bf16[16,4,64]{2,1,0:T(4,128)(2,1)} %bitcast.79), custom_call_target="tpu_custom_call" | custom-call | tf_op jit(solution)/shard_map/pallas_call | solution.py:83
  44.0 1.1 %convolution_convert_fusion = bf16[64,2048]{1,0:T(8,128)(2,1)S(1)} fusion(bf16[64,64]{1,0:T(8,128)(2,1)} %bitcast.78, bf16[1,64,2048]{2,1,0:T(8,128)(2,1)S(1)} %copy-done.1, s32[64]{0:T(128)S(1)} %fusion.58), kind=kOutput, calls=%fused_computation.4 | convolution fusion | flops 17440768 | bytes 532736 | tf_op jit(solution)/shard_map/dot_general | solution.py:222
  45.1 0.9 reshape.385.x_ref
  45.9 14.8 %shard_map.112 = bf16[32,2,2048]{2,1,0:T(2,128)(2,1)} custom-call(bf16[32,2,2048]{2,1,0:T(2,128)(2,1)} %reshape.385.x_ref), custom_call_target="tpu_custom_call" | custom-call | tf_op jit(solution)/shard_map/pallas_call | solution.py:83
  60.7 1.2 %convert_reduce_fusion = f32[2,2048]{1,0:T(2,128)S(1)} fusion(bf16[32,2,2048]{2,1,0:T(2,128)(2,1)} %shard_map.112), kind=kLoop, calls=%fused_computation.13 | loop fusion | flops 258048 | bytes 278528 | tf_op jit(solution)/shard_map/reduce_sum | solution.py:226
  61.9 0.1 multiply_reduce_fusion.2
  62.1 0.2 fusion.34
  62.3 0.7 fusion.36.x_ref
  63.0 13.3 %shard_map.113 = bf16[16,2,2048]{2,1,0:T(2,128)(2,1)} custom-call(bf16[2,2048]{1,0:T(2,128)(2,1)} %fusion.36.x_ref), custom_call_target="tpu_custom_call" | custom-call | tf_op jit(solution)/shard_map/pallas_call | solution.py:83
  76.3 1.0 %reshape.391 = bf16[32,2048,1]{1,0,2:T(8,128)(2,1)S(1)} reshape(bf16[16,2,2048]{2,1,0:T(2,128)(2,1)} %shard_map.113) | data formatting | bytes 262144 | tf_op jit(solution)/shard_map/reshape | solution.py:233
  77.3 3.0 %fusion = f32[32,2,512]{2,0,1:T(8,128)S(1)} fusion(bf16[32,2048,1]{1,0,2:T(8,128)(2,1)S(1)} %reshape.391, bf16[2048,2,512]{2,1,0:T(2,128)(2,1)} %param.17), kind=kOutput, calls=%fused_computation | convolution fusion | flops 134217728 | bytes 4456448 | tf_op jit(solution)/shard_map/nd,dgf->ngf/dot_general | solution.py:234
  80.3 0.5 convolution_convert_fusion.1
  80.7 0.8 reshape.387.x_ref
  81.5 10.5 %shard_map.114 = bf16[16,2,2048]{2,1,0:T(2,128)(2,1)} custom-call(bf16[16,2,2048]{2,1,0:T(2,128)(2,1)} %reshape.387.x_ref), custom_call_target="tpu_custom_call" | custom-call | tf_op jit(solution)/shard_map/pallas_call | solution.py:83
  92.0 1.0 %convert_reduce_fusion.1 = f32[2,2048]{1,0:T(2,128)S(1)} fusion(bf16[16,2,2048]{2,1,0:T(2,128)(2,1)} %shard_map.114), kind=kLoop, calls=%fused_computation.18 | loop fusion | flops 126976 | bytes 147456 | tf_op jit(solution)/shard_map/reduce_sum | solution.py:242
  93.0 0.1 multiply_reduce_fusion.1
  93.2 0.7 fusion.44
  (32 shorter events, 0.4 us)
Async XLA Ops:
  0.0 80.3 %copy-start = (bf16[512,2048]{1,0:T(8,128)(2,1)S(1)}, bf16[512,2048]{1,0:T(8,128)(2,1)}, u32[]{:S(2)}) copy-start(bf16[512,2048]{1,0:T(8,128)(2,1)} %param.18) | copy-start | bytes 6291460
  0.0 28.8 %copy-start.3 = (f32[2,256]{1,0:T(2,128)S(1)}, f32[2,256]{1,0:T(2,128)}, u32[]{:S(2)}) copy-start(f32[2,256]{1,0:T(2,128)} %param.13) | copy-start | bytes 6148
  33.2 10.7 %copy-start.1 = (bf16[1,64,2048]{2,1,0:T(8,128)(2,1)S(1)}, bf16[1,64,2048]{2,1,0:T(8,128)(2,1)}, u32[]{:S(2)}) copy-start(bf16[1,64,2048]{2,1,0:T(8,128)(2,1)} %param.16) | copy-start | bytes 786436
  33.8 28.2 %copy-start.2 = (bf16[4,1,2048]{2,0,1:T(4,128)(2,1)S(1)}, bf16[4,1,2048]{2,0,1:T(4,128)(2,1)}, u32[]{:S(2)}) copy-start(bf16[4,1,2048]{2,0,1:T(4,128)(2,1)} %param.11) | copy-start | bytes 49156

commit v2 on v1

--- a/solution.py
+++ b/solution.py
@@ -76,6 +76,8 @@
 
 
 def exchange(x, group, cid, bcast=False):
+    if not bcast:
+        return lax.all_to_all(x, group, 0, 0, tiled=True)
     n = 1
     for a in group:
         n *= lax.axis_size(a)

time: 94.7 us -> 105 us (1.11)
  Pallas kernels: 67.7 us -> 13.2 us
  blocking collectives: 0 us -> 22.4 us
  starting transfers between devices: 0 us -> 19.8 us
  waiting for transfers between devices: 0 us -> 15.7 us
  other arithmetic: 9.01 us -> 12.2 us
  local copies, waits for them, and re-layouts: 10.1 us -> 12.7 us
  matrix products: 6.84 us -> 8.1 us
    pallas_call x6 -> x1, Pallas kernels: 67.7 us -> 13.2 us  [exchange(): pl.pallas_call(functools.partial(exchange_kernel, group, bcast), out_shap...]
    all_to_all x0 -> x2, blocking collectives: none -> 22.4 us  [exchange(): return lax.all_to_all(x, group, 0, 0, tiled=True)]
    all_to_all x0 -> x3, starting transfers between devices: none -> 19.8 us  [exchange(): return lax.all_to_all(x, group, 0, 0, tiled=True)]
    all_to_all x0 -> x3, waiting for transfers between devices: none -> 15.7 us  [exchange(): return lax.all_to_all(x, group, 0, 0, tiled=True)]
    dot_general x1, matrix products: 0.42 us -> 1.76 us  [shards(): jnp.dot(weights.astype(jnp.bfloat16).reshape(rows_here * per_group, -1),...]
    convert_element_type x1, other arithmetic: 0.07 us -> 1.33 us  [shards(): value_new.astype(jnp.float32)[:, None, :]]
    concatenate x1, other arithmetic: 0.11 us -> 1.36 us  [rotate(): jnp.concatenate([first_half * cosines - second_half * sines, second_half...]
    slice x1, local copies, waits for them, and re-layouts: 1.98 us -> 3.22 us  [shards(): cached_keys = kv_cache[:, 0].reshape(pool_size * page_size, head_width)]
  transfers between devices with their start and end apart: 0 -> 3, of which waited for: 0 -> 3; matrix products, arithmetic and copies ran while one was open for 0% -> 8% of each run, Pallas kernels for 0% -> 0%
where the time goes in v2:
time: 105 us; the launch traced here: 104 us
  blocking collectives  22.4 us (21%)
  starting transfers between devices  19.8 us (19%)
  waiting for transfers between devices  15.7 us (15%)
  Pallas kernels  13.2 us (13%)
  local copies, waits for them, and re-layouts  12.7 us (12%)
  other arithmetic  12.2 us (12%)
  matrix products  8.1 us (8%)
    all_to_all x2, blocking collectives, exchange(): return lax.all_to_all(x, group, 0, 0, tiled=True)  22.4 us
    all_to_all x3, starting transfers between devices, exchange(): return lax.all_to_all(x, group, 0, 0, tiled=True)  19.8 us
    all_to_all x3, waiting for transfers between devices, exchange(): return lax.all_to_all(x, group, 0, 0, tiled=True)  15.7 us
    pallas_call x1, Pallas kernels, exchange(): pl.pallas_call(functools.partial(exchange_kernel, group, bcast), out_shap...  13.2 us
    slice x1, local copies, waits for them, and re-layouts, shards(): cached_keys = kv_cache[:, 0].reshape(pool_size * page_size, head_width)  3.22 us
    dot_general x1, matrix products, shards(): jnp.einsum('nd,dgf->ngf', ffn_rows, w_gateup, preferred_element_type=jnp....  3.01 us
  transfers between devices with their start and end apart: 3, of which 3 were waited for; matrix products, arithmetic and copies ran while one was open for 8% of the time, Pallas kernels for 0%

profile of v2, /device:TPU:1, one launch (start us, length us, event | category | flops | bytes accessed | tf_op | source)
XLA Modules:
  0.0 104.4 jit_solution(2608346628248913209)
XLA Ops:
  0.0 1.6 %fusion.71 = (f32[1,2048]{1,0:T(1,128)S(1)}, f32[1,2048]{1,0:T(1,128)}, f32[1,2048]{1,0:T(1,128)S(1)}, f32[1,2048]{1,0:T(1,128)}) fusion(f32[4,2048]{1,0:T(4,128)} %param.12), kind=kLoop, calls=%fused_computation.129 | loop fusion | bytes 65536 | tf_op jit(solution)/shard_map/slice | solution.py:234
  1.6 0.8 multiply_reduce_fusion
  2.5 1.4 %fusion.38 = bf16[16,4,128]{2,1,0:T(4,128)(2,1)} fusion(f32[16,128]{1,0:T(8,128)S(1)} %bitcast.83, f32[4]{0:T(128)S(1)} %add_rsqrt_fusion.6, bf16[4,1,2048]{2,0,1:T(4,128)(2,1)} %param.11), kind=kLoop, calls=%fused_computation.58 | loop fusion | flops 32768 | bytes 40976 | tf_op jit(solution)/shard_map/transpose | solution.py:146
  3.9 7.6 %all-to-all-start = ((bf16[16,4,128]{2,1,0:T(4,128)(2,1)}), bf16[16,4,128]{2,1,0:T(4,128)(2,1)S(1)}, u32[]{:S(2)}, u32[]{:S(2)}) async-start(bf16[16,4,128]{2,1,0:T(4,128)(2,1)} %fusion.38), calls=%async_computation | async-start | bytes 32768 | tf_op jit(solution)/shard_map/all_to_all | solution.py:80
  11.5 0.7 dynamic-slice_bitcast_fusion
  12.3 0.7 fusion.59
  13.0 0.1 select_reduce_fusion.2
  13.1 0.1 select_reduce_fusion.1
  13.5 0.1 broadcast_reduce_fusion
  14.1 0.7 multiply_cosine_fusion.1
  14.8 0.9 copy.21
  15.7 2.2 %all-to-all-done = bf16[16,4,128]{2,1,0:T(4,128)(2,1)S(1)} async-done(((bf16[16,4,128]{2,1,0:T(4,128)(2,1)}), bf16[16,4,128]{2,1,0:T(4,128)(2,1)S(1)}, u32[]{:S(2)}, u32[]{:S(2)}) %all-to-all-start) | async-done | bytes 16416 | tf_op jit(solution)/shard_map/all_to_all | solution.py:80
  17.9 1.2 %fusion.5 = f32[64,1536]{1,0:T(8,128)S(1)} fusion(bf16[64,128]{1,0:T(8,128)(2,1)S(1)} %bitcast.77, bf16[128,512]{1,0:T(8,128)(2,1)S(1)} %bitcast.75, bf16[128,1024]{1,0:T(8,128)(2,1)} %param.14, s32[64]{0:T(128)S(1)} %fusion.58), kind=kOutput, calls=%fused_computation.11 | convolution fusion | flops 27013120 | bytes 803072 | tf_op jit(solution)/shard_map/dot_general | solution.py:163
  19.1 0.9 reshape.382
  20.0 4.5 %all-to-all-start.1 = ((f32[16,4,1536]{2,1,0:T(4,128)}), f32[16,4,1536]{2,1,0:T(4,128)}, u32[]{:S(2)}, u32[]{:S(2)}) async-start(f32[16,4,1536]{2,1,0:T(4,128)} %reshape.382), calls=%async_computation.1 | async-start | bytes 786432 | tf_op jit(solution)/shard_map/all_to_all | solution.py:80
  24.5 0.6 fusion.72
  25.1 3.2 %fusion.70 = (bf16[43,1,64,256]{3,2,1,0:T(8,128)(2,1)S(1)}, bf16[43,1,64,256]{3,2,1,0:T(8,128)(2,1)}) fusion(bf16[43,2,64,256]{3,2,1,0:T(8,128)(2,1)} %param.19), kind=kLoop, calls=%fused_computation.128 | loop fusion | bytes 5636096 | tf_op jit(solution)/shard_map/slice | solution.py:190
  28.3 4.5 %all-to-all-done.1 = f32[16,4,1536]{2,1,0:T(4,128)} async-done(((f32[16,4,1536]{2,1,0:T(4,128)}), f32[16,4,1536]{2,1,0:T(4,128)}, u32[]{:S(2)}, u32[]{:S(2)}) %all-to-all-start.1) | async-done | bytes 393248 | tf_op jit(solution)/shard_map/all_to_all | solution.py:80
  32.9 1.1 %reduce_sum.139 = f32[4,1536]{1,0:T(4,128)S(1)} reduce(f32[16,4,1536]{2,1,0:T(4,128)} %all-to-all-done.1, f32[]{:T(128)} %constant.99.clone.1), dimensions={0}, to_apply=%region_5.6 | reduce | flops 92160 | bytes 417796 | tf_op jit(solution)/shard_map/reduce_sum | solution.py:165
  34.0 0.1 multiply_reduce_fusion.5
  34.1 0.6 slice.73
  34.7 1.3 %fusion.55 = (f32[4,256]{1,0:T(4,128)}, f32[4,1,256]{2,0,1:T(4,128)S(1)}) fusion(f32[4,1536]{1,0:T(4,128)S(1)} %reduce_sum.139, f32[4]{0:T(128)S(1)} %get-tuple-element.32, f32[256]{0:T(256)} %bitcast.85, f32[4]{0:T(128)S(1)} %get-tuple-element.33), kind=kLoop, calls=%fused_computation.95 | loop fusion | flops 5120 | bytes 17440 | tf_op jit(solution)/shard_map/convert_element_type | solution.py:214
  36.1 1.4 %fusion.57 = (bf16[4,128]{1,0:T(4,128)(2,1)}, bf16[4,128]{1,0:T(4,128)(2,1)}) fusion(f32[4,1,256]{2,0,1:T(4,128)S(1)} %get-tuple-element.21, f32[128]{0:T(128)} %copy-done.6, f32[4]{0:T(128)} %copy-done.7), kind=kLoop, calls=%fused_computation.110 | loop fusion | flops 4608 | bytes 6672 | tf_op jit(solution)/shard_map/concatenate | solution.py:110
  37.4 0.7 reshape.383
  38.3 0.7 maximum_convert_fusion
  38.9 0.8 multiply_multiply_fusion.1
  39.7 0.7 subtract_convert_fusion
  40.5 0.6 fusion.73
  41.1 0.2 fusion.11
  41.3 1.8 %fusion.6 = bf16[4,4,256]{2,1,0:T(4,128)(2,1)S(1)} fusion(bf16[2752,256,1]{1,0,2:T(8,128)(2,1)} %bitcast.74, f32[4,4,2752]{2,1,0:T(4,128)S(1)} %get-tuple-element.31, f32[4,4]{1,0:T(4,128)S(1)} %get-tuple-element.30, pred[4,2752]{1,0:T(4,128)(4,1)S(1)} %compare_and_fusion, f32[4,4]{1,0:T(4,128)S(1)} %get-tuple-element.9, f32[4,256]{1,0:T(4,128)} %get-tuple-element.20, ...), kind=kOutput, calls=%fused_computation.12 | convolution fusion | flops 22696960 | bytes 1608704 | tf_op jit(solution)/shard_map/dot_general | solution.py:202
  43.3 9.1 %all_to_all.25 = bf16[16,2,128]{2,1,0:T(2,128)(2,1)S(1)} all-to-all(bf16[16,2,128]{2,1,0:T(2,128)(2,1)S(1)} %reshape.394), channel_id=1, replica_groups=mesh['req'=16,'kv'=2,'hid'=8] {'req'}, dimensions={0} | all-to-all | bytes 16384 | tf_op jit(solution)/shard_map/all_to_all | solution.py:80
  52.4 1.0 %convolution_convert_fusion = bf16[64,2048]{1,0:T(8,128)(2,1)S(1)} fusion(bf16[64,64]{1,0:T(8,128)(2,1)S(1)} %bitcast.78, bf16[1,64,2048]{2,1,0:T(8,128)(2,1)S(1)} %copy-done.1, s32[64]{0:T(128)} %copy-done.5), kind=kOutput, calls=%fused_computation.4 | convolution fusion | flops 17440768 | bytes 532736 | tf_op jit(solution)/shard_map/dot_general | solution.py:224
  53.5 0.9 reshape.385
  54.4 7.7 %all-to-all-start.3 = ((bf16[32,2,2048]{2,1,0:T(2,128)(2,1)}), bf16[32,2,2048]{2,1,0:T(2,128)(2,1)S(1)}, u32[]{:S(2)}, u32[]{:S(2)}) async-start(bf16[32,2,2048]{2,1,0:T(2,128)(2,1)} %reshape.385), calls=%async_computation.3 | async-start | bytes 524288 | tf_op jit(solution)/shard_map/all_to_all | solution.py:80
  62.1 9.0 %all-to-all-done.3 = bf16[32,2,2048]{2,1,0:T(2,128)(2,1)S(1)} async-done(((bf16[32,2,2048]{2,1,0:T(2,128)(2,1)}), bf16[32,2,2048]{2,1,0:T(2,128)(2,1)S(1)}, u32[]{:S(2)}, u32[]{:S(2)}) %all-to-all-start.3) | async-done | bytes 262176 | tf_op jit(solution)/shard_map/all_to_all | solution.py:80
  71.1 0.2 convert_reduce_fusion
  71.3 0.1 multiply_reduce_fusion.2
  71.5 0.2 fusion.34
  71.7 0.7 fusion.36.x_ref
  72.4 13.2 %shard_map.109 = bf16[16,2,2048]{2,1,0:T(2,128)(2,1)} custom-call(bf16[2,2048]{1,0:T(2,128)(2,1)} %fusion.36.x_ref), custom_call_target="tpu_custom_call" | custom-call | tf_op jit(solution)/shard_map/pallas_call | solution.py:85
  85.5 1.0 reshape.391
  86.5 3.0 %fusion = f32[32,2,512]{2,0,1:T(8,128)S(1)} fusion(bf16[32,2048,1]{1,0,2:T(8,128)(2,1)S(1)} %reshape.391, bf16[2048,2,512]{2,1,0:T(2,128)(2,1)} %param.17), kind=kOutput, calls=%fused_computation | convolution fusion | flops 134217728 | bytes 4456448 | tf_op jit(solution)/shard_map/nd,dgf->ngf/dot_general | solution.py:236
  89.5 0.4 convolution_convert_fusion.1
  90.0 0.1 reshape.387
  90.1 13.3 %all_to_all.26 = bf16[16,2,2048]{2,1,0:T(2,128)(2,1)S(1)} all-to-all(bf16[16,2,2048]{2,1,0:T(2,128)(2,1)S(1)} %reshape.387), channel_id=1, replica_groups=mesh['req'=16,'kv'=2,'hid'=8] {'kv','hid'}, dimensions={0} | all-to-all | bytes 262144 | tf_op jit(solution)/shard_map/all_to_all | solution.py:80
  103.4 0.1 convert_reduce_fusion.1
  103.6 0.1 multiply_reduce_fusion.1
  103.7 0.7 fusion.44
  (47 shorter events, 1.2 us)
Async XLA Ops:
  0.0 89.5 %copy-start = (bf16[512,2048]{1,0:T(8,128)(2,1)S(1)}, bf16[512,2048]{1,0:T(8,128)(2,1)}, u32[]{:S(2)}) copy-start(bf16[512,2048]{1,0:T(8,128)(2,1)} %param.18) | copy-start | bytes 6291460
  0.0 24.5 %copy-start.8 = (f32[2,256]{1,0:T(2,128)S(1)}, f32[2,256]{1,0:T(2,128)}, u32[]{:S(2)}) copy-start(f32[2,256]{1,0:T(2,128)} %param.13) | copy-start | bytes 6148
  3.9 14.0 %all-to-all-start = ((bf16[16,4,128]{2,1,0:T(4,128)(2,1)}), bf16[16,4,128]{2,1,0:T(4,128)(2,1)S(1)}, u32[]{:S(2)}, u32[]{:S(2)}) async-start(bf16[16,4,128]{2,1,0:T(4,128)(2,1)} %fusion.38), calls=%async_computation | async-start | bytes 32768 | tf_op jit(solution)/shard_map/all_to_all | solution.py:80
  11.5 3.3 %copy-start.6 = (f32[128]{0:T(128)}, f32[128]{0:T(128)S(1)}, u32[]{:S(2)}) copy-start(f32[128]{0:T(128)S(1)} %multiply_power_fusion) | copy-start | bytes 1540
  12.2 12.3 %copy-start.5 = (s32[64]{0:T(128)}, s32[64]{0:T(128)S(1)}, u32[]{:S(2)}) copy-start(s32[64]{0:T(128)S(1)} %fusion.58) | copy-start | bytes 772
  13.5 1.3 %copy-start.7 = (f32[4]{0:T(128)}, f32[4]{0:T(128)S(1)}, u32[]{:S(2)}) copy-start(f32[4]{0:T(128)S(1)} %convert_element_type.91) | copy-start | bytes 52
  20.0 12.9 %all-to-all-start.1 = ((f32[16,4,1536]{2,1,0:T(4,128)}), f32[16,4,1536]{2,1,0:T(4,128)}, u32[]{:S(2)}, u32[]{:S(2)}) async-start(f32[16,4,1536]{2,1,0:T(4,128)} %reshape.382), calls=%async_computation.1 | async-start | bytes 786432 | tf_op jit(solution)/shard_map/all_to_all | solution.py:80
  41.1 11.4 %copy-start.1 = (bf16[1,64,2048]{2,1,0:T(8,128)(2,1)S(1)}, bf16[1,64,2048]{2,1,0:T(8,128)(2,1)}, u32[]{:S(2)}) copy-start(bf16[1,64,2048]{2,1,0:T(8,128)(2,1)} %param.16) | copy-start | bytes 786436
  41.1 21.1 %copy-start.2 = (bf16[4,1,2048]{2,0,1:T(4,128)(2,1)S(1)}, bf16[4,1,2048]{2,0,1:T(4,128)(2,1)}, u32[]{:S(2)}) copy-start(bf16[4,1,2048]{2,0,1:T(4,128)(2,1)} %param.11) | copy-start | bytes 49156
  41.1 30.4 %copy-start.3 = (f32[1,2048]{1,0:T(1,128)S(1)}, f32[1,2048]{1,0:T(1,128)}, u32[]{:S(2)}) copy-start(f32[1,2048]{1,0:T(1,128)} %get-tuple-element.17) | copy-start | bytes 24580
  54.4 16.8 %all-to-all-start.3 = ((bf16[32,2,2048]{2,1,0:T(2,128)(2,1)}), bf16[32,2,2048]{2,1,0:T(2,128)(2,1)S(1)}, u32[]{:S(2)}, u32[]{:S(2)}) async-start(bf16[32,2,2048]{2,1,0:T(2,128)(2,1)} %reshape.385), calls=%async_computation.3 | async-start | bytes 524288 | tf_op jit(solution)/shard_map/all_to_all | solution.py:80
  89.5 14.2 %copy-start.4 = (f32[1,2048]{1,0:T(1,128)S(1)}, f32[1,2048]{1,0:T(1,128)}, u32[]{:S(2)}) copy-start(f32[1,2048]{1,0:T(1,128)} %get-tuple-element.19) | copy-start | bytes 24580

commit v3 on v1

--- a/solution.py
+++ b/solution.py
@@ -159,8 +159,9 @@
         [w_query, key_value_weight.reshape(key_value_weight.shape[0], -1)], axis=1
     )
     partial = jnp.dot(columns_pooled, projection, preferred_element_type=jnp.float32)
-    gathered = exchange(partial.reshape(req_total, rows_here, -1), ("req",), 1)
-    summed = jnp.sum(gathered, axis=0)
+    qkv_width = partial.shape[1]
+    gathered = exchange(partial.reshape(req_total, 8, -1), ("req",), 1)
+    summed = jnp.sum(gathered.reshape(req_total, rows_here, qkv_width), axis=0)
 
     mine = lax.dynamic_slice_in_dim(order, req_position * rows_here, rows_here, 0)
     my_lengths = jnp.sum(jnp.where(mine, group_lengths[None, :], 0), axis=1)
@@ -220,17 +221,20 @@
         jnp.bfloat16
     )
     proj_partial = jnp.dot(att_natural, output_weight[0], preferred_element_type=jnp.float32)
-    proj_partial = proj_partial.astype(jnp.bfloat16).reshape(
-        req_total * kv_total, half_rows, model_width
-    )
+    proj_partial = proj_partial.astype(jnp.bfloat16).reshape(req_total * kv_total, 16, -1)
     projected = jnp.sum(
-        exchange(proj_partial, ("req", "kv"), 3).astype(jnp.float32), axis=0
+        exchange(proj_partial, ("req", "kv"), 3)
+        .reshape(req_total * kv_total, half_rows, model_width)
+        .astype(jnp.float32),
+        axis=0,
     )
 
     residual = lax.dynamic_slice_in_dim(own_rows, kv_position * half_rows, half_rows, 0)
     middle = (residual + rms_scale(projected, gains[1])).astype(jnp.bfloat16)
     ffn_input = rms_scale(middle.astype(jnp.float32), gains[2]).astype(jnp.bfloat16)
-    ffn_rows = exchange(ffn_input, ("kv", "hid"), 4, bcast=True).reshape(-1, model_width)
+    ffn_rows = exchange(ffn_input.reshape(16, -1), ("kv", "hid"), 4, bcast=True).reshape(
+        -1, model_width
+    )
     gate_up = jnp.einsum(
         "nd,dgf->ngf", ffn_rows, w_gateup, preferred_element_type=jnp.float32
     )
@@ -238,8 +242,13 @@
     ffn_partial = jnp.dot(hidden, w_down, preferred_element_type=jnp.float32).astype(
         jnp.bfloat16
     )
-    ffn_partial = ffn_partial.reshape(kv_total * hid_total, half_rows, model_width)
-    ffn_sum = jnp.sum(exchange(ffn_partial, ("kv", "hid"), 5).astype(jnp.float32), axis=0)
+    ffn_partial = ffn_partial.reshape(kv_total * hid_total, 16, -1)
+    ffn_sum = jnp.sum(
+        exchange(ffn_partial, ("kv", "hid"), 5)
+        .reshape(kv_total * hid_total, half_rows, model_width)
+        .astype(jnp.float32),
+        axis=0,
+    )
     result = (middle.astype(jnp.float32) + rms_scale(ffn_sum, gains[3])).astype(jnp.bfloat16)
     return result[:, None, :]
 

time: 94.7 us -> 94.7 us (level)
    reshape x4 -> x5, local copies, waits for them, and re-layouts: 3.44 us -> 3.92 us  [the longest x1 0.97 us: shards(): exchange(ffn_input.reshape(16, -1), ('kv', 'hid'), 4, bcast=True)]
where the time goes in v3:
time: 94.7 us; the launch traced here: 93.9 us
  Pallas kernels  67.7 us (71%)
  local copies, waits for them, and re-layouts  10.8 us (11%)
  other arithmetic  8.3 us (9%)
  matrix products  6.84 us (7%)
    pallas_call x6, Pallas kernels, exchange(): pl.pallas_call(functools.partial(exchange_kernel, group, bcast), out_shap...  67.7 us
    dot_general x1, matrix products, shards(): jnp.einsum('nd,dgf->ngf', ffn_rows, w_gateup, preferred_element_type=jnp....  3.01 us
    slice x1, local copies, waits for them, and re-layouts, shards(): cached_keys = kv_cache[:, 0].reshape(pool_size * page_size, head_width)  1.98 us

profile of v3, /device:TPU:1, one launch (start us, length us, event | category | flops | bytes accessed | tf_op | source)
XLA Modules:
  0.0 93.9 jit_solution(2644072365321394357)
XLA Ops:
  0.0 0.9 dynamic-slice_bitcast_fusion
  0.9 0.9 %fusion.71 = (f32[1,2048]{1,0:T(1,128)S(1)}, f32[1,2048]{1,0:T(1,128)S(1)}, f32[1,2048]{1,0:T(1,128)S(1)}, f32[1,2048]{1,0:T(1,128)S(1)}) fusion(f32[4,2048]{1,0:T(4,128)} %param.12), kind=kLoop, calls=%fused_computation.129 | loop fusion | bytes 65536 | tf_op jit(solution)/shard_map/slice | solution.py:234
  1.9 0.8 multiply_reduce_fusion
  2.7 1.4 %fusion.38.x_ref = bf16[16,4,128]{2,1,0:T(4,128)(2,1)} fusion(f32[16,128]{1,0:T(8,128)S(1)} %bitcast.83, f32[4]{0:T(128)S(1)} %add_rsqrt_fusion.6, bf16[4,1,2048]{2,0,1:T(4,128)(2,1)} %param.11), kind=kLoop, calls=%fused_computation.58 | loop fusion | flops 32768 | bytes 40976 | tf_op jit(solution)/shard_map/transpose | solution.py:144
  4.1 10.5 %shard_map.109 = bf16[16,4,128]{2,1,0:T(4,128)(2,1)} custom-call(bf16[16,4,128]{2,1,0:T(4,128)(2,1)} %fusion.38.x_ref), custom_call_target="tpu_custom_call" | custom-call | tf_op jit(solution)/shard_map/pallas_call | solution.py:83
  14.6 0.9 copy.19
  15.5 1.3 %fusion.5 = f32[64,1536]{1,0:T(8,128)S(1)} fusion(bf16[64,128]{1,0:T(8,128)(2,1)} %bitcast.77, bf16[128,512]{1,0:T(8,128)(2,1)S(1)} %bitcast.75, bf16[128,1024]{1,0:T(8,128)(2,1)} %param.14, s32[64]{0:T(128)S(1)} %fusion.58), kind=kOutput, calls=%fused_computation.11 | convolution fusion | flops 27013120 | bytes 803072 | tf_op jit(solution)/shard_map/dot_general | solution.py:161
  16.8 0.8 reshape.393.x_ref
  17.6 9.9 %shard_map.110 = f32[16,8,768]{2,1,0:T(8,128)} custom-call(f32[16,8,768]{2,1,0:T(8,128)} %reshape.393.x_ref), custom_call_target="tpu_custom_call" | custom-call | tf_op jit(solution)/shard_map/pallas_call | solution.py:83
  27.5 1.0 %reduce_sum.159 = f32[8,768]{1,0:T(8,128)S(1)} reduce(f32[16,8,768]{2,1,0:T(8,128)} %shard_map.110, f32[]{:T(128)} %constant.99.clone.1), dimensions={0}, to_apply=%region_5.6 | reduce | flops 92160 | bytes 417796 | tf_op jit(solution)/shard_map/reduce_sum | solution.py:164
  28.5 0.1 multiply_reduce_fusion.5
  28.8 0.7 fusion.59
  29.5 0.1 select_reduce_fusion.2
  29.6 0.1 fusion.57
  29.8 0.1 multiply_cosine_fusion.1
  29.9 0.1 multiply_reduce_fusion.4
  30.1 0.1 multiply_reduce_fusion.3
  30.2 0.1 select_reduce_fusion.1
  30.4 0.1 select_reduce_fusion
  30.5 0.1 broadcast_reduce_fusion
  30.8 0.1 fusion.26
  30.9 0.1 and.56
  31.0 0.1 and.57
  31.2 2.0 %fusion.70 = (bf16[43,1,64,256]{3,2,1,0:T(8,128)(2,1)S(1)}, bf16[43,1,64,256]{3,2,1,0:T(8,128)(2,1)S(1)}) fusion(bf16[43,2,64,256]{3,2,1,0:T(8,128)(2,1)} %param.19), kind=kLoop, calls=%fused_computation.128 | loop fusion | bytes 5636096 | tf_op jit(solution)/shard_map/slice | solution.py:189
  33.2 0.6 fusion.73
  33.8 0.2 fusion.11
  34.0 0.4 fusion.6
  34.4 0.1 reshape_reshape.3
  34.5 0.6 copy.23
  35.1 8.7 %shard_map.111 = bf16[16,4,64]{2,1,0:T(4,128)(2,1)} custom-call(bf16[16,4,64]{2,1,0:T(4,128)(2,1)} %bitcast.79), custom_call_target="tpu_custom_call" | custom-call | tf_op jit(solution)/shard_map/pallas_call | solution.py:83
  43.9 1.1 %convolution_convert_fusion = bf16[64,2048]{1,0:T(8,128)(2,1)S(1)} fusion(bf16[64,64]{1,0:T(8,128)(2,1)} %bitcast.78, bf16[1,64,2048]{2,1,0:T(8,128)(2,1)S(1)} %copy-done.1, s32[64]{0:T(128)S(1)} %fusion.58), kind=kOutput, calls=%fused_computation.4 | convolution fusion | flops 17440768 | bytes 532736 | tf_op jit(solution)/shard_map/dot_general | solution.py:223
  45.0 0.8 reshape.396.x_ref
  45.8 14.8 %shard_map.112 = bf16[32,16,256]{2,1,0:T(8,128)(2,1)} custom-call(bf16[32,16,256]{2,1,0:T(8,128)(2,1)} %reshape.396.x_ref), custom_call_target="tpu_custom_call" | custom-call | tf_op jit(solution)/shard_map/pallas_call | solution.py:83
  60.6 1.0 %convert_reduce_fusion = f32[16,256]{1,0:T(8,128)S(1)} fusion(bf16[32,16,256]{2,1,0:T(8,128)(2,1)} %shard_map.112), kind=kLoop, calls=%fused_computation.13 | loop fusion | flops 258048 | bytes 278528 | tf_op jit(solution)/shard_map/reduce_sum | solution.py:225
  61.6 0.1 multiply_reduce_fusion.2
  61.8 0.1 reduce_sum.170
  62.0 0.2 fusion.34
  62.3 0.6 reshape.397.x_ref
  62.9 13.3 %shard_map.113 = bf16[16,16,256]{2,1,0:T(8,128)(2,1)} custom-call(bf16[16,256]{1,0:T(8,128)(2,1)} %reshape.397.x_ref), custom_call_target="tpu_custom_call" | custom-call | tf_op jit(solution)/shard_map/pallas_call | solution.py:83
  76.2 1.0 %reshape.403 = bf16[32,2048,1]{1,0,2:T(8,128)(2,1)S(1)} reshape(bf16[16,16,256]{2,1,0:T(8,128)(2,1)} %shard_map.113) | data formatting | bytes 262144 | tf_op jit(solution)/shard_map/reshape | solution.py:235
  77.1 3.0 %fusion = f32[32,2,512]{2,0,1:T(8,128)S(1)} fusion(bf16[32,2048,1]{1,0,2:T(8,128)(2,1)S(1)} %reshape.403, bf16[2048,2,512]{2,1,0:T(2,128)(2,1)} %param.17), kind=kOutput, calls=%fused_computation | convolution fusion | flops 134217728 | bytes 4456448 | tf_op jit(solution)/shard_map/nd,dgf->ngf/dot_general | solution.py:238
  80.2 0.5 convolution_convert_fusion.1
  80.6 0.7 reshape.399.x_ref
  81.3 10.6 %shard_map.114 = bf16[16,16,256]{2,1,0:T(8,128)(2,1)} custom-call(bf16[16,16,256]{2,1,0:T(8,128)(2,1)} %reshape.399.x_ref), custom_call_target="tpu_custom_call" | custom-call | tf_op jit(solution)/shard_map/pallas_call | solution.py:83
  91.9 0.9 convert_reduce_fusion.1
  92.9 0.1 multiply_reduce_fusion.1
  93.0 0.1 reduce_sum.176
  93.2 0.7 fusion.44
  (40 shorter events, 0.9 us)
Async XLA Ops:
  0.0 80.2 %copy-start = (bf16[512,2048]{1,0:T(8,128)(2,1)S(1)}, bf16[512,2048]{1,0:T(8,128)(2,1)}, u32[]{:S(2)}) copy-start(bf16[512,2048]{1,0:T(8,128)(2,1)} %param.18) | copy-start | bytes 6291460
  0.0 28.7 %copy-start.3 = (f32[2,256]{1,0:T(2,128)S(1)}, f32[2,256]{1,0:T(2,128)}, u32[]{:S(2)}) copy-start(f32[2,256]{1,0:T(2,128)} %param.13) | copy-start | bytes 6148
  33.2 10.7 %copy-start.1 = (bf16[1,64,2048]{2,1,0:T(8,128)(2,1)S(1)}, bf16[1,64,2048]{2,1,0:T(8,128)(2,1)}, u32[]{:S(2)}) copy-start(bf16[1,64,2048]{2,1,0:T(8,128)(2,1)} %param.16) | copy-start | bytes 786436
  33.8 28.2 %copy-start.2 = (bf16[4,1,2048]{2,0,1:T(4,128)(2,1)S(1)}, bf16[4,1,2048]{2,0,1:T(4,128)(2,1)}, u32[]{:S(2)}) copy-start(bf16[4,1,2048]{2,0,1:T(4,128)(2,1)} %param.11) | copy-start | bytes 49156

commit v4 on v1

--- a/solution.py
+++ b/solution.py
@@ -90,6 +90,170 @@
     )(x)
 
 
+def start_copies(group, src_of, dst_ref, send_sem, recv_sem):
+    sizes, me, n = group_layout(group)
+    copies = []
+    for s in range(1, n):
+        peer = lax.rem(me + s, n)
+        copy = pltpu.make_async_remote_copy(
+            src_ref=src_of(peer),
+            dst_ref=dst_ref.at[me],
+            send_sem=send_sem.at[s],
+            recv_sem=recv_sem.at[s],
+            device_id=device_of(group, sizes, peer),
+            device_id_type=MESH,
+        )
+        copy.start()
+        copies.append(copy)
+
+    def finish():
+        for s in range(1, n):
+            copies[s - 1].wait_send()
+            origin = lax.rem(me + n - s, n)
+            pltpu.make_async_remote_copy(
+                src_ref=src_of(origin),
+                dst_ref=dst_ref.at[origin],
+                send_sem=send_sem.at[s],
+                recv_sem=recv_sem.at[s],
+                device_id=device_of(group, sizes, origin),
+                device_id_type=MESH,
+            ).wait_recv()
+
+    return me, finish
+
+
+def rms_rows(value_entries, gain_row):
+    mean_square = jnp.mean(value_entries * value_entries, axis=-1, keepdims=True)
+    return value_entries * lax.rsqrt(mean_square + eps_norm) * gain_row
+
+
+def tail_kernel(
+    att_ref, unperm_ref, wout_ref, resid_ref, gains_ref, wgu_hbm, wd_hbm,
+    out_ref,
+    y_att, att_rows, w_pad, send_proj, y_proj, ffn_src, y_ffn, ffn_rows, ffn_out,
+    send_red, y_red, wgu_v, wd_v,
+    att_send, att_recv, proj_send, proj_recv, ffn_send, ffn_recv, red_send, red_recv, w_sem,
+):
+    wgu_copy = pltpu.make_async_copy(wgu_hbm, wgu_v, w_sem.at[0])
+    wd_copy = pltpu.make_async_copy(wd_hbm, wd_v, w_sem.at[1])
+    wgu_copy.start()
+    wd_copy.start()
+
+    wide = ("req", "kv")
+    narrow = ("kv", "hid")
+    wide_sizes, wide_me, wide_n = group_layout(wide)
+    narrow_sizes, narrow_me, narrow_n = group_layout(narrow)
+    half = narrow_n // 2
+    barrier = pltpu.get_barrier_semaphore()
+    for s in range(1, wide_n):
+        peer = lax.rem(wide_me + s, wide_n)
+        pl.semaphore_signal(
+            barrier, inc=1, device_id=device_of(wide, wide_sizes, peer), device_id_type=MESH
+        )
+    for s in range(1, narrow_n):
+        if s == half:
+            continue
+        peer = lax.rem(narrow_me + s, narrow_n)
+        pl.semaphore_signal(
+            barrier, inc=1, device_id=device_of(narrow, narrow_sizes, peer), device_id_type=MESH
+        )
+    pl.semaphore_wait(barrier, wide_n - 1 + narrow_n - 2)
+
+    att_me, att_finish = start_copies(("req",), lambda k: att_ref.at[k], y_att, att_send, att_recv)
+    y_att[att_me] = att_ref[att_me]
+    att_rows[...] = jnp.zeros_like(att_rows)
+    w_pad[...] = jnp.zeros_like(w_pad)
+    rows_w = wout_ref.shape[0]
+    w_pad[0:rows_w, :] = wout_ref[...]
+    att_finish()
+    n_req, per_pool, slice_width = y_att.shape
+    for k in range(n_req):
+        att_rows[8 * k : 8 * k + per_pool, 0:slice_width] = y_att[k].astype(jnp.float32)
+    att_nat = jnp.dot(
+        unperm_ref[...], att_rows[...].astype(jnp.bfloat16), preferred_element_type=jnp.float32
+    ).astype(jnp.bfloat16)
+    proj = jnp.dot(att_nat, w_pad[...], preferred_element_type=jnp.float32)
+    n_wide, owned, width = send_proj.shape
+    for q in range(n_wide):
+        send_proj[q] = proj[owned * q : owned * (q + 1)].astype(jnp.bfloat16)
+
+    proj_me, proj_finish = start_copies(wide, lambda k: send_proj.at[k], y_proj, proj_send, proj_recv)
+    y_proj[proj_me] = send_proj[proj_me]
+    proj_finish()
+    projected = y_proj[0].astype(jnp.float32)
+    for k in range(1, n_wide):
+        projected = projected + y_proj[k].astype(jnp.float32)
+    middle = (resid_ref[...] + rms_rows(projected, gains_ref[1:2, :])).astype(jnp.bfloat16)
+    ffn_src[...] = rms_rows(middle.astype(jnp.float32), gains_ref[2:3, :]).astype(jnp.bfloat16)
+
+    ffn_me, ffn_finish = start_copies(narrow, lambda k: ffn_src, y_ffn, ffn_send, ffn_recv)
+    y_ffn[ffn_me] = ffn_src[...]
+    ffn_finish()
+    for k in range(narrow_n):
+        ffn_rows[owned * k : owned * (k + 1), :] = y_ffn[k].astype(jnp.float32)
+    wgu_copy.wait()
+    wd_copy.wait()
+    gate_up = jnp.dot(
+        ffn_rows[...].astype(jnp.bfloat16), wgu_v[...], preferred_element_type=jnp.float32
+    )
+    hidden_width = wd_v.shape[0]
+    hidden = (
+        jax.nn.gelu(gate_up[:, :hidden_width], approximate=True) * gate_up[:, hidden_width:]
+    ).astype(jnp.bfloat16)
+    ffn_out[...] = jnp.dot(hidden, wd_v[...], preferred_element_type=jnp.float32)
+    for k in range(narrow_n):
+        send_red[k] = ffn_out[owned * k : owned * (k + 1), :].astype(jnp.bfloat16)
+
+    red_me, red_finish = start_copies(narrow, lambda k: send_red.at[k], y_red, red_send, red_recv)
+    y_red[red_me] = send_red[red_me]
+    red_finish()
+    ffn_sum = y_red[0].astype(jnp.float32)
+    for k in range(1, narrow_n):
+        ffn_sum = ffn_sum + y_red[k].astype(jnp.float32)
+    out_ref[...] = (middle.astype(jnp.float32) + rms_rows(ffn_sum, gains_ref[3:4, :])).astype(
+        out_ref.dtype
+    )
+
+
+def tail(send_att, unperm, wout, residual, gains, wgu, wd, cid):
+    n_req = lax.axis_size("req")
+    n_wide = n_req * lax.axis_size("kv")
+    n_narrow = lax.axis_size("kv") * lax.axis_size("hid")
+    owned, width = residual.shape
+    vmem = pl.BlockSpec(memory_space=pltpu.VMEM)
+    anywhere = pl.BlockSpec(memory_space=pl.ANY)
+    dma = pltpu.SemaphoreType.DMA
+    return pl.pallas_call(
+        tail_kernel,
+        out_shape=jax.ShapeDtypeStruct((owned, width), jnp.bfloat16),
+        in_specs=[vmem, vmem, vmem, vmem, vmem, anywhere, anywhere],
+        out_specs=vmem,
+        scratch_shapes=[
+            pltpu.VMEM(send_att.shape, jnp.bfloat16),
+            pltpu.VMEM((8 * n_req, 128), jnp.float32),
+            pltpu.VMEM((128, width), jnp.bfloat16),
+            pltpu.VMEM((n_wide, owned, width), jnp.bfloat16),
+            pltpu.VMEM((n_wide, owned, width), jnp.bfloat16),
+            pltpu.VMEM((owned, width), jnp.bfloat16),
+            pltpu.VMEM((n_narrow, owned, width), jnp.bfloat16),
+            pltpu.VMEM((n_narrow * owned, width), jnp.float32),
+            pltpu.VMEM((n_narrow * owned, width), jnp.float32),
+            pltpu.VMEM((n_narrow, owned, width), jnp.bfloat16),
+            pltpu.VMEM((n_narrow, owned, width), jnp.bfloat16),
+            pltpu.VMEM(wgu.shape, jnp.bfloat16),
+            pltpu.VMEM(wd.shape, jnp.bfloat16),
+            dma((n_req,)), dma((n_req,)),
+            dma((n_wide,)), dma((n_wide,)),
+            dma((n_narrow,)), dma((n_narrow,)),
+            dma((n_narrow,)), dma((n_narrow,)),
+            dma((2,)),
+        ],
+        compiler_params=pltpu.CompilerParams(
+            collective_id=cid, has_side_effects=True, vmem_limit_bytes=48 * 1024 * 1024
+        ),
+    )(send_att, unperm, wout, residual, gains, wgu, wd)
+
+
 def rms_scale(value_entries, gain_row):
     mean_square = jnp.mean(value_entries * value_entries, axis=-1, keepdims=True)
     return value_entries * lax.rsqrt(mean_square + eps_norm) * gain_row
@@ -215,32 +379,21 @@
 
     slice_width = output_weight.shape[1]
     send_att = attended.reshape(rows_here, req_total, slice_width).transpose(1, 0, 2)
-    got_att = exchange(send_att, ("req",), 2).reshape(request_count, slice_width)
-    att_natural = jnp.dot(order_b.T, got_att, preferred_element_type=jnp.float32).astype(
-        jnp.bfloat16
-    )
-    proj_partial = jnp.dot(att_natural, output_weight[0], preferred_element_type=jnp.float32)
-    proj_partial = proj_partial.astype(jnp.bfloat16).reshape(
-        req_total * kv_total, half_rows, model_width
-    )
-    projected = jnp.sum(
-        exchange(proj_partial, ("req", "kv"), 3).astype(jnp.float32), axis=0
-    )
-
+    unperm = order.T.reshape(request_count, req_total, rows_here)
+    unperm = jnp.pad(unperm, ((0, 0), (0, 0), (0, 8 - rows_here)))
+    unperm = unperm.reshape(request_count, 8 * req_total).astype(jnp.bfloat16)
     residual = lax.dynamic_slice_in_dim(own_rows, kv_position * half_rows, half_rows, 0)
-    middle = (residual + rms_scale(projected, gains[1])).astype(jnp.bfloat16)
-    ffn_input = rms_scale(middle.astype(jnp.float32), gains[2]).astype(jnp.bfloat16)
-    ffn_rows = exchange(ffn_input, ("kv", "hid"), 4, bcast=True).reshape(-1, model_width)
-    gate_up = jnp.einsum(
-        "nd,dgf->ngf", ffn_rows, w_gateup, preferred_element_type=jnp.float32
-    )
-    hidden = (jax.nn.gelu(gate_up[:, 0], approximate=True) * gate_up[:, 1]).astype(jnp.bfloat16)
-    ffn_partial = jnp.dot(hidden, w_down, preferred_element_type=jnp.float32).astype(
-        jnp.bfloat16
-    )
-    ffn_partial = ffn_partial.reshape(kv_total * hid_total, half_rows, model_width)
-    ffn_sum = jnp.sum(exchange(ffn_partial, ("kv", "hid"), 5).astype(jnp.float32), axis=0)
-    result = (middle.astype(jnp.float32) + rms_scale(ffn_sum, gains[3])).astype(jnp.bfloat16)
+    hidden_width = w_down.shape[0]
+    result = tail(
+        send_att,
+        unperm,
+        output_weight[0],
+        residual,
+        gains,
+        w_gateup.reshape(model_width, 2 * hidden_width),
+        w_down,
+        2,
+    )
     return result[:, None, :]
 
 

time: 94.7 us -> 76.9 us (0.81)
  Pallas kernels: 67.7 us -> 56.9 us
  matrix products: 6.84 us -> 2.43 us
  other arithmetic: 9.01 us -> 5.76 us
  local copies, waits for them, and re-layouts: 10.1 us -> 11.2 us
    pallas_call x6 -> x2, Pallas kernels: 67.7 us -> 20.4 us  [exchange(): pl.pallas_call(functools.partial(exchange_kernel, group, bcast), out_shap...]
    pallas_call x0 -> x1, Pallas kernels: none -> 36.5 us  [tail(): pl.pallas_call(tail_kernel, out_shape=jax.ShapeDtypeStruct((owned, width)...]
    unnamed x9 -> x13, local copies, waits for them, and re-layouts: 0.94 us -> 7.01 us
    dot_general x3 -> x0, matrix products: 4.57 us -> none  [the longest x1 3.01 us: shards(): jnp.einsum('nd,dgf->ngf', ffn_rows, w_gateup, preferred_element_type=jnp....]
    reshape x3 -> x0, local copies, waits for them, and re-layouts: 2.59 us -> none  [the longest x1 0.96 us: shards(): exchange(ffn_input, ('kv', 'hid'), 4, bcast=True).reshape(-1, model_width)]
    reduce_sum x2 -> x0, other arithmetic: 2.2 us -> none  [the longest x1 1.18 us: shards(): jnp.sum(exchange(proj_partial, ('req', 'kv'), 3).astype(jnp.float32), axi...]
    slice x1, local copies, waits for them, and re-layouts: 1.98 us -> 0.34 us  [shards(): cached_keys = kv_cache[:, 0].reshape(pool_size * page_size, head_width)]
where the time goes in v4:
time: 76.9 us; the launch traced here: 76.4 us
  Pallas kernels  56.9 us (74%)
  local copies, waits for them, and re-layouts  11.2 us (15%)
  other arithmetic  5.76 us (7%)
  matrix products  2.43 us (3%)
    pallas_call x1, Pallas kernels, tail(): pl.pallas_call(tail_kernel, out_shape=jax.ShapeDtypeStruct((owned, width)...  36.5 us
    pallas_call x2, Pallas kernels, exchange(): pl.pallas_call(functools.partial(exchange_kernel, group, bcast), out_shap...  20.4 us
    unnamed x13, local copies, waits for them, and re-layouts  7.01 us

profile of v4, /device:TPU:1, one launch (start us, length us, event | category | flops | bytes accessed | tf_op | source)
XLA Modules:
  0.0 76.4 jit_solution(2675393161338515859)
XLA Ops:
  0.0 0.0 copy-start
  0.0 0.7 fusion.33
  0.7 0.8 %multiply_reduce_fusion = f32[4]{0:T(128)S(1)} fusion(bf16[4,1,2048]{2,0,1:T(4,128)(2,1)} %param.11), kind=kLoop, calls=%fused_computation.27 | loop fusion | flops 24572 | bytes 16400 | tf_op jit(solution)/shard_map/reduce_sum | solution.py:258
  1.6 0.8 %fusion.40 = (f32[1,256]{1,0:T(1,128)S(1)}, f32[1,256]{1,0:T(1,128)S(1)}) fusion(f32[2,256]{1,0:T(2,128)} %param.13), kind=kLoop, calls=%fused_computation.89 | loop fusion | bytes 4096 | tf_op jit(solution)/shard_map/slice | solution.py:338
  2.4 0.8 slice.40
  3.1 1.4 %fusion.18.x_ref = bf16[16,4,128]{2,1,0:T(4,128)(2,1)} fusion(bf16[4,1,2048]{2,0,1:T(4,128)(2,1)} %param.11, f32[16,128]{1,0:T(8,128)S(1)} %bitcast.64, f32[4]{0:T(128)S(1)} %add_rsqrt_fusion.3), kind=kLoop, calls=%fused_computation.29 | loop fusion | flops 32768 | bytes 40976 | tf_op jit(solution)/shard_map/transpose | solution.py:308
  4.5 10.5 %shard_map.109 = bf16[16,4,128]{2,1,0:T(4,128)(2,1)} custom-call(bf16[16,4,128]{2,1,0:T(4,128)(2,1)} %fusion.18.x_ref), custom_call_target="tpu_custom_call" | custom-call | tf_op jit(solution)/shard_map/pallas_call | solution.py:83
  15.0 0.0 copy-done
  15.1 0.1 broadcast_compare_fusion
  15.2 0.1 select_reduce_fusion.2
  15.3 0.1 select_reduce_fusion.1
  15.5 0.1 select_reduce_fusion
  15.6 0.1 fusion.14
  15.7 0.1 multiply_cosine_fusion.1
  15.8 0.1 broadcast_reduce_fusion
  15.9 0.1 add.121
  16.0 0.1 and.56
  16.1 0.1 and.57
  16.2 0.1 copy.17.unperm_ref
  16.3 0.1 add.123
  16.4 0.1 compare_and_fusion
  16.5 0.7 convert_element_type.76
  17.2 0.9 %copy.18 = bf16[16,8,2,256]{3,1,2,0:T(8,128)(2,1)S(1)} copy(bf16[16,8,2,256]{3,2,1,0:T(2,128)(2,1)} %bitcast.62) | data formatting | bytes 262144
  18.2 0.0 copy-start.4
  18.2 1.4 %fusion.3 = f32[64,1536]{1,0:T(8,128)S(1)} fusion(bf16[64,128]{1,0:T(8,128)(2,1)} %bitcast.63, bf16[128,512]{1,0:T(8,128)(2,1)S(1)} %bitcast.61, bf16[128,1024]{1,0:T(8,128)(2,1)} %param.14, s32[64]{0:T(128)S(1)} %fusion.32), kind=kOutput, calls=%fused_computation.6 | convolution fusion | flops 27013120 | bytes 803072 | tf_op jit(solution)/shard_map/dot_general | solution.py:325
  19.6 0.8 %reshape.367.x_ref = f32[16,4,1536]{2,1,0:T(4,128)} reshape(f32[64,1536]{1,0:T(8,128)S(1)} %fusion.3) | data formatting | bytes 786432 | tf_op jit(solution)/shard_map/reshape | solution.py:326
  20.4 9.9 %shard_map.110 = f32[16,4,1536]{2,1,0:T(4,128)} custom-call(f32[16,4,1536]{2,1,0:T(4,128)} %reshape.367.x_ref), custom_call_target="tpu_custom_call" | custom-call | tf_op jit(solution)/shard_map/pallas_call | solution.py:83
  30.4 1.1 %reduce_sum.94 = f32[4,1536]{1,0:T(4,128)S(1)} reduce(f32[16,4,1536]{2,1,0:T(4,128)} %shard_map.110, f32[]{:T(128)} %constant.91.clone.1), dimensions={0}, to_apply=%region_5.6 | reduce | flops 92160 | bytes 417796 | tf_op jit(solution)/shard_map/reduce_sum | solution.py:327
  31.4 0.1 multiply_reduce_fusion.3
  31.6 0.1 fusion.29
  31.7 0.1 fusion.31
  31.8 0.1 multiply_reduce_fusion.2
  31.9 0.1 multiply_multiply_fusion
  32.0 0.1 multiply_reduce_fusion.1
  32.1 0.0 copy-done.4
  32.1 0.3 fusion.39
  32.5 0.6 fusion.41
  33.1 0.2 fusion.8
  33.3 0.4 fusion.4
  33.7 0.1 reshape_reshape.3
  33.8 0.0 copy-start.1
  33.8 0.0 copy-start.2
  33.9 0.0 copy-start.3
  33.9 5.5 %copy.19 = bf16[256,8,2,512]{3,1,2,0:T(8,128)(2,1)} copy(bf16[256,8,2,512]{3,2,1,0:T(2,128)(2,1)} %bitcast.59) | data formatting | bytes 8388608
  39.3 0.0 copy-done.1
  39.3 0.0 copy-done.3
  39.3 36.5 %shard_map.111 = bf16[2,2048]{1,0:T(2,128)(2,1)S(1)} custom-call(bf16[16,4,64]{2,1,0:T(4,128)(2,1)S(1)} %bitcast.55, bf16[64,128]{1,0:T(8,128)(2,1)S(1)} %copy.17.unperm_ref, bf16[64,2048]{1,0:T(8,128)(2,1)S(1)} %bitcast.54, f32[2,2048]{1,0:T(2,128)S(1)} %dynamic-slice_bitcast_fusion.resid_ref, f32[4,2048]{1,0:T(4,128)S(1)} %copy-done.3, ...), custom_call_target="tpu_custom_call" | custom-call | tf_op jit(solution)/shard_map/pallas_call | solution.py:226
  75.8 0.6 copy.23
  (22 shorter events, 0.2 us)
Async XLA Ops:
  0.0 15.0 %copy-start = (s32[64,8,32]{0,2,1:T(8,128)S(1)}, s32[64,8,32]{0,2,1:T(8,128)}, u32[]{:S(2)}) copy-start(s32[64,8,32]{0,2,1:T(8,128)} %param.21) | copy-start | bytes 196612
  18.2 13.9 %copy-start.4 = (bf16[43,2,64,256]{3,2,1,0:T(8,128)(2,1)S(1)}, bf16[43,2,64,256]{3,2,1,0:T(8,128)(2,1)}, u32[]{:S(2)}) copy-start(bf16[43,2,64,256]{3,2,1,0:T(8,128)(2,1)} %param.19) | copy-start | bytes 8454148
  33.8 5.5 %copy-start.1 = (bf16[512,2048]{1,0:T(8,128)(2,1)S(1)}, bf16[512,2048]{1,0:T(8,128)(2,1)}, u32[]{:S(2)}) copy-start(bf16[512,2048]{1,0:T(8,128)(2,1)} %wd_hbm.1) | copy-start | bytes 6291460
  33.8 5.5 %copy-start.2 = (bf16[1,64,2048]{2,1,0:T(8,128)(2,1)S(1)}, bf16[1,64,2048]{2,1,0:T(8,128)(2,1)}, u32[]{:S(2)}) copy-start(bf16[1,64,2048]{2,1,0:T(8,128)(2,1)} %param.16) | copy-start | bytes 786436
  33.9 5.5 %copy-start.3 = (f32[4,2048]{1,0:T(4,128)S(1)}, f32[4,2048]{1,0:T(4,128)}, u32[]{:S(2)}) copy-start(f32[4,2048]{1,0:T(4,128)} %gains_ref.1) | copy-start | bytes 98308

commit v5 on v4

--- a/solution.py
+++ b/solution.py
@@ -127,15 +127,23 @@
     return value_entries * lax.rsqrt(mean_square + eps_norm) * gain_row
 
 
-def tail_kernel(
-    att_ref, unperm_ref, wout_ref, resid_ref, gains_ref, wgu_hbm, wd_hbm,
+def layer_kernel(
+    tok_ref, gains_ref, qkg_ref, order_ref, projw_ref, trig_ref, mask_ref, kv_hbm,
+    unperm_ref, wout_ref, resid_ref, wgu_hbm, wd_hbm,
     out_ref,
-    y_att, att_rows, w_pad, send_proj, y_proj, ffn_src, y_ffn, ffn_rows, ffn_out,
+    tok_src, y_tok, tok_rows, send_qkv, y_qkv, keys_v, vals_v, q16, k16, v16, comb,
+    send_att, y_att, att_rows, w_pad, send_proj, y_proj, ffn_src, y_ffn, ffn_rows, ffn_out,
     send_red, y_red, wgu_v, wd_v,
+    tok_send, tok_recv, qkv_send, qkv_recv,
     att_send, att_recv, proj_send, proj_recv, ffn_send, ffn_recv, red_send, red_recv, w_sem,
 ):
-    wgu_copy = pltpu.make_async_copy(wgu_hbm, wgu_v, w_sem.at[0])
-    wd_copy = pltpu.make_async_copy(wd_hbm, wd_v, w_sem.at[1])
+    n_pages = kv_hbm.shape[0]
+    keys_copy = pltpu.make_async_copy(kv_hbm.at[:, 0], keys_v.at[pl.ds(0, n_pages)], w_sem.at[0])
+    vals_copy = pltpu.make_async_copy(kv_hbm.at[:, 1], vals_v.at[pl.ds(0, n_pages)], w_sem.at[1])
+    wgu_copy = pltpu.make_async_copy(wgu_hbm, wgu_v, w_sem.at[2])
+    wd_copy = pltpu.make_async_copy(wd_hbm, wd_v, w_sem.at[3])
+    keys_copy.start()
+    vals_copy.start()
     wgu_copy.start()
     wd_copy.start()
 
@@ -157,16 +165,93 @@
         pl.semaphore_signal(
             barrier, inc=1, device_id=device_of(narrow, narrow_sizes, peer), device_id_type=MESH
         )
+
+    n_req, per_pool, feature_width = tok_src.shape
+    normed = rms_rows(tok_ref[...].astype(jnp.float32), gains_ref[0:1, :]).astype(jnp.bfloat16)
+    for k in range(n_req):
+        tok_src[k] = normed[:, feature_width * k : feature_width * (k + 1)]
+    tok_rows[...] = jnp.zeros_like(tok_rows)
     pl.semaphore_wait(barrier, wide_n - 1 + narrow_n - 2)
 
-    att_me, att_finish = start_copies(("req",), lambda k: att_ref.at[k], y_att, att_send, att_recv)
-    y_att[att_me] = att_ref[att_me]
+    tok_me, tok_finish = start_copies(("req",), lambda k: tok_src.at[k], y_tok, tok_send, tok_recv)
+    y_tok[tok_me] = tok_src[tok_me]
+    tok_finish()
+    for k in range(n_req):
+        tok_rows[8 * k : 8 * k + per_pool, :] = y_tok[k].astype(jnp.float32)
+    pooled = jnp.dot(
+        order_ref[...], tok_rows[...].astype(jnp.bfloat16), preferred_element_type=jnp.float32
+    ).astype(jnp.bfloat16)
+    partial = jnp.dot(pooled, projw_ref[...], preferred_element_type=jnp.float32)
+    for k in range(n_req):
+        send_qkv[k] = partial[8 * k : 8 * k + per_pool]
+
+    qkv_me, qkv_finish = start_copies(("req",), lambda k: send_qkv.at[k], y_qkv, qkv_send, qkv_recv)
+    y_qkv[qkv_me] = send_qkv[qkv_me]
+    qkv_finish()
+    summed = y_qkv[0]
+    for k in range(1, n_req):
+        summed = summed + y_qkv[k]
+    cosines = trig_ref[0]
+    sines = trig_ref[1]
+    head_width = q16.shape[1]
+    half_width = head_width // 2
+
+    def rot(v):
+        a = v[:, :half_width]
+        b = v[:, half_width:]
+        return jnp.concatenate([a * cosines - b * sines, b * cosines + a * sines], axis=-1)
+
+    per_group = q16.shape[0] // per_pool
+    for h in range(per_group):
+        qh = rot(rms_rows(summed[:, head_width * h : head_width * (h + 1)], qkg_ref[0:1, :]))
+        q16[per_pool * h : per_pool * (h + 1), :] = qh.astype(jnp.bfloat16).astype(jnp.float32)
+    split_at = per_group * head_width
+    kn = rot(rms_rows(summed[:, split_at : split_at + head_width], qkg_ref[1:2, :]))
+    kn = kn.astype(jnp.bfloat16).astype(jnp.float32)
+    vn = rms_rows(summed[:, split_at + head_width :], 1.0)
+    vn = vn.astype(jnp.bfloat16).astype(jnp.float32)
+    for h in range(per_group):
+        k16[per_pool * h : per_pool * (h + 1), :] = kn
+        v16[per_pool * h : per_pool * (h + 1), :] = vn
+
+    keys_copy.wait()
+    vals_copy.wait()
+    keys_v[n_pages] = jnp.zeros(keys_v.shape[1:], keys_v.dtype)
+    vals_v[n_pages] = jnp.zeros(vals_v.shape[1:], vals_v.dtype)
+    total_pos = keys_v.shape[0] * keys_v.shape[1]
+    keys = keys_v[...].reshape(total_pos, head_width)
+    vals = vals_v[...].reshape(total_pos, head_width)
+    scale_factor = head_width ** (-0.5)
+    q_f = q16[...]
+    scores = lax.dot_general(
+        q_f.astype(jnp.bfloat16), keys, (((1,), (1,)), ((), ())),
+        preferred_element_type=jnp.float32,
+    ) * scale_factor
+    live = mask_ref[...] != 0
+    masked = jnp.where(live, scores, neg_large)
+    highest_cached = jnp.max(masked, axis=1, keepdims=True)
+    weights = jnp.where(live, jnp.exp(masked - highest_cached), 0.0)
+    totals = jnp.sum(weights, axis=1, keepdims=True)
+    weighted = jnp.dot(weights.astype(jnp.bfloat16), vals, preferred_element_type=jnp.float32)
+    own_score = jnp.sum(q_f * k16[...], axis=1, keepdims=True) * scale_factor
+    highest = jnp.maximum(highest_cached, own_score)
+    old_scale = jnp.exp(highest_cached - highest)
+    new_scale = jnp.exp(own_score - highest)
+    combined = (weighted * old_scale + new_scale * v16[...]) / (totals * old_scale + new_scale)
+    comb[...] = combined.astype(jnp.bfloat16).astype(jnp.float32)
+    slice_width = send_att.shape[2]
+    per_head = head_width // slice_width
+    for k in range(n_req):
+        h, m = divmod(k, per_head)
+        send_att[k] = comb[per_pool * h : per_pool * (h + 1), slice_width * m : slice_width * (m + 1)].astype(jnp.bfloat16)
+
+    att_me, att_finish = start_copies(("req",), lambda k: send_att.at[k], y_att, att_send, att_recv)
+    y_att[att_me] = send_att[att_me]
     att_rows[...] = jnp.zeros_like(att_rows)
     w_pad[...] = jnp.zeros_like(w_pad)
     rows_w = wout_ref.shape[0]
     w_pad[0:rows_w, :] = wout_ref[...]
     att_finish()
-    n_req, per_pool, slice_width = y_att.shape
     for k in range(n_req):
         att_rows[8 * k : 8 * k + per_pool, 0:slice_width] = y_att[k].astype(jnp.float32)
     att_nat = jnp.dot(
@@ -215,44 +300,67 @@
     )
 
 
-def tail(send_att, unperm, wout, residual, gains, wgu, wd, cid):
+def layer(tok, gains, qk_gains, order_pad, projw, trig, mask16, kv_cache,
+          unperm, wout, residual, wgu, wd, cid):
     n_req = lax.axis_size("req")
     n_wide = n_req * lax.axis_size("kv")
     n_narrow = lax.axis_size("kv") * lax.axis_size("hid")
     owned, width = residual.shape
+    per_pool = tok.shape[0]
+    feature_width = width // n_req
+    qkv_width = projw.shape[1]
+    n_pages, _, page_size, head_width = kv_cache.shape
+    slice_width = wout.shape[0]
+    rows16 = mask16.shape[0]
     vmem = pl.BlockSpec(memory_space=pltpu.VMEM)
     anywhere = pl.BlockSpec(memory_space=pl.ANY)
     dma = pltpu.SemaphoreType.DMA
+    f32 = jnp.float32
+    bf16 = jnp.bfloat16
     return pl.pallas_call(
-        tail_kernel,
-        out_shape=jax.ShapeDtypeStruct((owned, width), jnp.bfloat16),
-        in_specs=[vmem, vmem, vmem, vmem, vmem, anywhere, anywhere],
+        layer_kernel,
+        out_shape=jax.ShapeDtypeStruct((owned, width), bf16),
+        in_specs=[vmem] * 7 + [anywhere] + [vmem] * 3 + [anywhere, anywhere],
         out_specs=vmem,
         scratch_shapes=[
-            pltpu.VMEM(send_att.shape, jnp.bfloat16),
-            pltpu.VMEM((8 * n_req, 128), jnp.float32),
-            pltpu.VMEM((128, width), jnp.bfloat16),
-            pltpu.VMEM((n_wide, owned, width), jnp.bfloat16),
-            pltpu.VMEM((n_wide, owned, width), jnp.bfloat16),
-            pltpu.VMEM((owned, width), jnp.bfloat16),
-            pltpu.VMEM((n_narrow, owned, width), jnp.bfloat16),
-            pltpu.VMEM((n_narrow * owned, width), jnp.float32),
-            pltpu.VMEM((n_narrow * owned, width), jnp.float32),
-            pltpu.VMEM((n_narrow, owned, width), jnp.bfloat16),
-            pltpu.VMEM((n_narrow, owned, width), jnp.bfloat16),
-            pltpu.VMEM(wgu.shape, jnp.bfloat16),
-            pltpu.VMEM(wd.shape, jnp.bfloat16),
+            pltpu.VMEM((n_req, per_pool, feature_width), bf16),
+            pltpu.VMEM((n_req, per_pool, feature_width), bf16),
+            pltpu.VMEM((8 * n_req, feature_width), f32),
+            pltpu.VMEM((n_req, per_pool, qkv_width), f32),
+            pltpu.VMEM((n_req, per_pool, qkv_width), f32),
+            pltpu.VMEM((n_pages + 1, page_size, head_width), bf16),
+            pltpu.VMEM((n_pages + 1, page_size, head_width), bf16),
+            pltpu.VMEM((rows16, head_width), f32),
+            pltpu.VMEM((rows16, head_width), f32),
+            pltpu.VMEM((rows16, head_width), f32),
+            pltpu.VMEM((rows16, head_width), f32),
+            pltpu.VMEM((n_req, per_pool, slice_width), bf16),
+            pltpu.VMEM((n_req, per_pool, slice_width), bf16),
+            pltpu.VMEM((8 * n_req, 128), f32),
+            pltpu.VMEM((128, width), bf16),
+            pltpu.VMEM((n_wide, owned, width), bf16),
+            pltpu.VMEM((n_wide, owned, width), bf16),
+            pltpu.VMEM((owned, width), bf16),
+            pltpu.VMEM((n_narrow, owned, width), bf16),
+            pltpu.VMEM((n_narrow * owned, width), f32),
+            pltpu.VMEM((n_narrow * owned, width), f32),
+            pltpu.VMEM((n_narrow, owned, width), bf16),
+            pltpu.VMEM((n_narrow, owned, width), bf16),
+            pltpu.VMEM(wgu.shape, bf16),
+            pltpu.VMEM(wd.shape, bf16),
+            dma((n_req,)), dma((n_req,)),
+            dma((n_req,)), dma((n_req,)),
             dma((n_req,)), dma((n_req,)),
             dma((n_wide,)), dma((n_wide,)),
             dma((n_narrow,)), dma((n_narrow,)),
             dma((n_narrow,)), dma((n_narrow,)),
-            dma((2,)),
+            dma((4,)),
         ],
         compiler_params=pltpu.CompilerParams(
             collective_id=cid, has_side_effects=True, vmem_limit_bytes=48 * 1024 * 1024
         ),
-    )(send_att, unperm, wout, residual, gains, wgu, wd)
-
+    )(tok, gains, qk_gains, order_pad, projw, trig, mask16, kv_cache,
+      unperm, wout, residual, wgu, wd)
 
 def rms_scale(value_entries, gain_row):
     mean_square = jnp.mean(value_entries * value_entries, axis=-1, keepdims=True)
@@ -302,11 +410,7 @@
     request_count = rows_here * req_total
     feature_width = w_query.shape[0]
 
-    own_rows = tokens[:, 0, :].astype(jnp.float32)
-    normed = rms_scale(own_rows, gains[0]).astype(jnp.bfloat16)
-
-    send_tokens = normed.reshape(rows_here, req_total, feature_width).transpose(1, 0, 2)
-    columns = exchange(send_tokens, ("req",), 0).reshape(request_count, feature_width)
+    own_rows = tokens[:, 0, :]
 
     group_lengths = lax.dynamic_index_in_dim(lengths, hid_position, axis=1, keepdims=False)
     group_table = lax.dynamic_index_in_dim(page_table, hid_position, axis=1, keepdims=False)
@@ -314,29 +418,26 @@
     pool_of = (group_table[:, 0] // pool_size) // hid_total
     pool_pos = pool_of * rows_here + request_ids % rows_here
     order = pool_pos[None, :] == request_ids[:, None]
-    order_b = order.astype(jnp.bfloat16)
-    columns_pooled = jnp.dot(order_b, columns, preferred_element_type=jnp.float32).astype(
-        jnp.bfloat16
-    )
+    pad_to = 8 - rows_here
+    order_pad = order.reshape(req_total, rows_here, req_total, rows_here)
+    order_pad = jnp.pad(order_pad, ((0, 0), (0, pad_to), (0, 0), (0, pad_to)))
+    order_pad = order_pad.reshape(8 * req_total, 8 * req_total).astype(jnp.bfloat16)
+    unperm = order.T.reshape(request_count, req_total, rows_here)
+    unperm = jnp.pad(unperm, ((0, 0), (0, 0), (0, pad_to)))
+    unperm = unperm.reshape(request_count, 8 * req_total).astype(jnp.bfloat16)
 
     projection = jnp.concatenate(
         [w_query, key_value_weight.reshape(key_value_weight.shape[0], -1)], axis=1
     )
-    partial = jnp.dot(columns_pooled, projection, preferred_element_type=jnp.float32)
-    gathered = exchange(partial.reshape(req_total, rows_here, -1), ("req",), 1)
-    summed = jnp.sum(gathered, axis=0)
 
     mine = lax.dynamic_slice_in_dim(order, req_position * rows_here, rows_here, 0)
     my_lengths = jnp.sum(jnp.where(mine, group_lengths[None, :], 0), axis=1)
     my_tables = jnp.sum(jnp.where(mine[:, :, None], group_table[None, :, :], 0), axis=1)
-
     position = my_lengths.astype(jnp.float32)
-    split_at = per_group * head_width
-    query = summed[:, :split_at].reshape(rows_here, per_group, head_width)
-    query = rotate(rms_scale(query, qk_gains[0]), position).astype(jnp.bfloat16)
-    key_part = summed[:, split_at : split_at + head_width][:, None, :]
-    key_new = rotate(rms_scale(key_part, qk_gains[1]), position)[:, 0].astype(jnp.bfloat16)
-    value_new = rms_scale(summed[:, split_at + head_width :], 1.0).astype(jnp.bfloat16)
+    half_width = head_width // 2
+    frequency = rope_base ** (-jnp.arange(half_width, dtype=jnp.float32) * 2.0 / head_width)
+    angles = position[:, None] * frequency
+    trig = jnp.stack([jnp.cos(angles), jnp.sin(angles)])
 
     slot_base = (req_position * hid_total + hid_position) * pool_size
     local = my_tables - slot_base
@@ -347,52 +448,27 @@
     page_of = jnp.sum(jnp.where(match, page_ids[None, :, None], 0), axis=(0, 1))
     cache_pos = page_of[:, None] * page_size + jnp.arange(page_size, dtype=jnp.int32)[None, :]
     live = owner_hit[:, :, None] & (cache_pos[None] < my_lengths[:, None, None])
-    live = live.reshape(rows_here, 1, pool_size * page_size)
-
-    cached_keys = kv_cache[:, 0].reshape(pool_size * page_size, head_width)
-    cached_values = kv_cache[:, 1].reshape(pool_size * page_size, head_width)
-    scale_factor = head_width ** (-0.5)
-    scores = jnp.dot(
-        query.reshape(rows_here * per_group, head_width),
-        cached_keys.T,
-        preferred_element_type=jnp.float32,
-    ).reshape(rows_here, per_group, -1) * scale_factor
-    masked = jnp.where(live, scores, neg_large)
-    highest_cached = jnp.max(masked, axis=2)
-    weights = jnp.where(live, jnp.exp(masked - highest_cached[..., None]), 0.0)
-    totals = jnp.sum(weights, axis=2)
-    weighted = jnp.dot(
-        weights.astype(jnp.bfloat16).reshape(rows_here * per_group, -1),
-        cached_values,
-        preferred_element_type=jnp.float32,
-    ).reshape(rows_here, per_group, head_width)
-    query_f = query.astype(jnp.float32)
-    own_score = jnp.sum(query_f * key_new.astype(jnp.float32)[:, None, :], axis=-1) * scale_factor
-    highest = jnp.maximum(highest_cached, own_score)
-    old_scale = jnp.exp(highest_cached - highest)
-    new_scale = jnp.exp(own_score - highest)
-    combined = (
-        weighted * old_scale[..., None]
-        + new_scale[..., None] * value_new.astype(jnp.float32)[:, None, :]
-    ) / (totals * old_scale + new_scale)[..., None]
-    attended = combined.astype(jnp.bfloat16).reshape(rows_here, per_group * head_width)
-
-    slice_width = output_weight.shape[1]
-    send_att = attended.reshape(rows_here, req_total, slice_width).transpose(1, 0, 2)
-    unperm = order.T.reshape(request_count, req_total, rows_here)
-    unperm = jnp.pad(unperm, ((0, 0), (0, 0), (0, 8 - rows_here)))
-    unperm = unperm.reshape(request_count, 8 * req_total).astype(jnp.bfloat16)
+    live = live.reshape(rows_here, pool_size * page_size)
+    live = jnp.pad(live, ((0, 0), (0, page_size)))
+    mask16 = jnp.tile(live, (per_group, 1)).astype(jnp.int32)
+
     residual = lax.dynamic_slice_in_dim(own_rows, kv_position * half_rows, half_rows, 0)
     hidden_width = w_down.shape[0]
-    result = tail(
-        send_att,
+    result = layer(
+        own_rows,
+        gains,
+        qk_gains,
+        order_pad,
+        projection,
+        trig,
+        mask16,
+        kv_cache,
         unperm,
         output_weight[0],
-        residual,
-        gains,
+        residual.astype(jnp.float32),
         w_gateup.reshape(model_width, 2 * hidden_width),
         w_down,
-        2,
+        0,
     )
     return result[:, None, :]
 

time: 76.9 us -> 64 us (0.83)
  Pallas kernels: 56.9 us -> 50.2 us
  matrix products: 2.43 us -> 0 us
  other arithmetic: 5.76 us -> 3.54 us
  local copies, waits for them, and re-layouts: 11.2 us -> 9.78 us
    pallas_call x3 -> x1, Pallas kernels: 56.9 us -> 50.2 us  [layer(): pl.pallas_call(layer_kernel, out_shape=jax.ShapeDtypeStruct((owned, width...]
    reduce_sum x6 -> x0, other arithmetic: 2.49 us -> none  [the longest x3 1.08 us: rms_scale(): jnp.mean(value_entries * value_entries, axis=-1, keepdims=True)]
    dot_general x3 -> x0, matrix products: 2.43 us -> none  [the longest x1 1.42 us: shards(): jnp.dot(columns_pooled, projection, preferred_element_type=jnp.float32)]
    slice x4 -> x0, local copies, waits for them, and re-layouts: 1.87 us -> none  [the longest x1 0.77 us: shards(): qk_gains[1]]
    transpose x1 -> x0, other arithmetic: 1.39 us -> none  [shards(): normed.reshape(rows_here, req_total, feature_width).transpose(1, 0, 2)]
    reshape x2 -> x0, local copies, waits for them, and re-layouts: 0.87 us -> none  [the longest x1 0.85 us: shards(): gathered = exchange(partial.reshape(req_total, rows_here, -1), ('req',), 1)]
    concatenate x1, other arithmetic: 0.11 us -> 0.98 us  [shards(): jnp.concatenate([w_query, key_value_weight.reshape(key_value_weight.shape...]
    unnamed x13 -> x17, local copies, waits for them, and re-layouts: 7.01 us -> 7.21 us
where the time goes in v5:
time: 64 us; the launch traced here: 63.8 us
  Pallas kernels  50.2 us (78%)
  local copies, waits for them, and re-layouts  9.78 us (15%)
  other arithmetic  3.54 us (6%)
    pallas_call x1, Pallas kernels, layer(): pl.pallas_call(layer_kernel, out_shape=jax.ShapeDtypeStruct((owned, width...  50.2 us
    unnamed x17, local copies, waits for them, and re-layouts  7.21 us

profile of v5, /device:TPU:1, one launch (start us, length us, event | category | flops | bytes accessed | tf_op | source)
XLA Modules:
  0.0 63.8 jit_solution(155016576110796595)
XLA Ops:
  0.0 0.0 copy-start
  0.0 0.7 %fusion.7 = s32[64]{0:T(128)S(1)} fusion(s32[64,8]{0,1:T(8,128)} %param.20, s32[]{:T(128)S(6)} %select_n.60), kind=kLoop, calls=%fused_computation.42 | loop fusion | bytes 516 | tf_op jit(solution)/shard_map/jit(_where)/broadcast_in_dim | solution.py:434
  0.7 0.2 copy-done
  1.0 0.5 broadcast.258
  1.5 0.7 %reduce.9 = s32[64]{0:T(128)S(1)} reduce(s32[64,1]{0,1:T(1,128)S(1)} %get-tuple-element.8, s32[]{:T(128)} %broadcast.258), dimensions={1}, to_apply=%slice_divide_fusion.reduce_sub_computation | reduce | bytes 516 | tf_op jit(solution)/shard_map/jit(floor_divide)/div | solution.py:418
  2.2 0.1 select_reduce_fusion.2
  2.3 0.1 select_reduce_fusion.1
  2.4 0.1 select_reduce_fusion
  2.5 0.1 fusion
  2.7 0.1 and.62
  2.7 0.1 multiply_cosine_fusion
  2.9 0.1 div.42
  3.0 0.1 broadcast_compare_fusion.1
  3.1 0.7 %bitcast_convert_fusion.resid_ref = f32[2,2048]{1,0:T(2,128)S(1)} fusion(bf16[4,1,2048]{2,0,1:T(4,128)(2,1)} %param.11, s32[]{:T(128)S(6)} %select_n.71), kind=kLoop, calls=%fused_computation.23 | loop fusion | flops 4096 | bytes 24580 | tf_op jit(solution)/shard_map/convert_element_type | solution.py:468
  3.8 0.1 broadcast_reduce_fusion
  4.0 0.1 add.88
  4.0 0.1 and.68
  4.1 0.1 and.69
  4.2 0.1 copy.15.unperm_ref
  4.4 0.1 add.90
  4.4 0.1 compare_and_fusion
  4.6 0.1 broadcast_compare_fusion
  4.7 0.9 %copy.16 = bf16[16,8,2,256]{3,1,2,0:T(8,128)(2,1)S(1)} copy(bf16[16,8,2,256]{3,2,1,0:T(2,128)(2,1)} %bitcast.33) | data formatting | bytes 262144
  5.7 0.1 convert_element_type.37.mask_ref
  5.7 1.0 %pad_maximum_fusion.projw_ref = bf16[128,1536]{1,0:T(8,128)(2,1)S(1)} fusion(bf16[128,512]{1,0:T(8,128)(2,1)S(1)} %bitcast.32, bf16[128,1024]{1,0:T(8,128)(2,1)} %param.14), kind=kLoop, calls=%fused_computation.1 | loop fusion | flops 786432 | bytes 786432 | tf_op jit(solution)/shard_map/concatenate | solution.py:429
  6.7 0.1 pad_convert_fusion
  6.8 0.5 reshape.254.order_ref
  7.4 0.0 copy-start.1
  7.4 0.0 copy-start.2
  7.4 0.0 copy-start.3
  7.4 0.0 copy-start.4
  7.4 0.0 copy-start.5
  7.4 0.0 copy-start.6
  7.4 5.5 %copy.17 = bf16[256,8,2,512]{3,1,2,0:T(8,128)(2,1)} copy(bf16[256,8,2,512]{3,2,1,0:T(2,128)(2,1)} %bitcast.31) | data formatting | bytes 8388608
  12.9 0.0 copy-done.1
  12.9 0.0 copy-done.2
  12.9 0.0 copy-done.3
  12.9 0.0 copy-done.4
  12.9 0.0 copy-done.5
  12.9 0.0 copy-done.6
  12.9 50.2 %shard_map.109 = bf16[2,2048]{1,0:T(2,128)(2,1)S(1)} custom-call(bf16[4,2048]{1,0:T(4,128)(2,1)S(1)} %bitcast.28, f32[4,2048]{1,0:T(4,128)S(1)} %copy-done.5, f32[2,256]{1,0:T(2,128)S(1)} %copy-done.6, bf16[128,128]{1,0:T(8,128)(2,1)S(1)} %reshape.254.order_ref, bf16[128,1536]{1,0:T(8,128)(2,1)S(1)} %pad_maximum_fusion.projw_ref, ...), custom_call_target="tpu_custom_call" | custom-call | tf_op jit(solution)/shard_map/pallas_call | solution.py:320
  63.2 0.6 copy.19
  (14 shorter events, 0.2 us)
Async XLA Ops:
  0.0 0.9 %copy-start = (s32[64,8,32]{0,2,1:T(8,128)S(1)}, s32[64,8,32]{0,2,1:T(8,128)}, u32[]{:S(2)}) copy-start(s32[64,8,32]{0,2,1:T(8,128)} %param.21) | copy-start | bytes 196612
  7.4 5.5 %copy-start.1 = (bf16[43,2,64,256]{3,2,1,0:T(8,128)(2,1)S(1)}, bf16[43,2,64,256]{3,2,1,0:T(8,128)(2,1)}, u32[]{:S(2)}) copy-start(bf16[43,2,64,256]{3,2,1,0:T(8,128)(2,1)} %kv_hbm.1) | copy-start | bytes 8454148
  7.4 5.5 %copy-start.2 = (bf16[512,2048]{1,0:T(8,128)(2,1)S(1)}, bf16[512,2048]{1,0:T(8,128)(2,1)}, u32[]{:S(2)}) copy-start(bf16[512,2048]{1,0:T(8,128)(2,1)} %wd_hbm.1) | copy-start | bytes 6291460
  7.4 5.5 %copy-start.3 = (bf16[1,64,2048]{2,1,0:T(8,128)(2,1)S(1)}, bf16[1,64,2048]{2,1,0:T(8,128)(2,1)}, u32[]{:S(2)}) copy-start(bf16[1,64,2048]{2,1,0:T(8,128)(2,1)} %param.16) | copy-start | bytes 786436
  7.4 5.5 %copy-start.4 = (bf16[4,1,2048]{2,0,1:T(4,128)(2,1)S(1)}, bf16[4,1,2048]{2,0,1:T(4,128)(2,1)}, u32[]{:S(2)}) copy-start(bf16[4,1,2048]{2,0,1:T(4,128)(2,1)} %param.11) | copy-start | bytes 49156
  7.4 5.5 %copy-start.5 = (f32[4,2048]{1,0:T(4,128)S(1)}, f32[4,2048]{1,0:T(4,128)}, u32[]{:S(2)}) copy-start(f32[4,2048]{1,0:T(4,128)} %gains_ref.1) | copy-start | bytes 98308
  7.4 5.5 %copy-start.6 = (f32[2,256]{1,0:T(2,128)S(1)}, f32[2,256]{1,0:T(2,128)}, u32[]{:S(2)}) copy-start(f32[2,256]{1,0:T(2,128)} %qkg_ref.1) | copy-start | bytes 6148

commit v6 on v5

--- a/solution.py
+++ b/solution.py
@@ -129,7 +129,7 @@
 
 def layer_kernel(
     tok_ref, gains_ref, qkg_ref, order_ref, projw_ref, trig_ref, mask_ref, kv_hbm,
-    unperm_ref, wout_ref, resid_ref, wgu_hbm, wd_hbm,
+    unperm_ref, wout_ref, resid_ref, wgu_ref, wd_hbm,
     out_ref,
     tok_src, y_tok, tok_rows, send_qkv, y_qkv, keys_v, vals_v, q16, k16, v16, comb,
     send_att, y_att, att_rows, w_pad, send_proj, y_proj, ffn_src, y_ffn, ffn_rows, ffn_out,
@@ -140,11 +140,9 @@
     n_pages = kv_hbm.shape[0]
     keys_copy = pltpu.make_async_copy(kv_hbm.at[:, 0], keys_v.at[pl.ds(0, n_pages)], w_sem.at[0])
     vals_copy = pltpu.make_async_copy(kv_hbm.at[:, 1], vals_v.at[pl.ds(0, n_pages)], w_sem.at[1])
-    wgu_copy = pltpu.make_async_copy(wgu_hbm, wgu_v, w_sem.at[2])
     wd_copy = pltpu.make_async_copy(wd_hbm, wd_v, w_sem.at[3])
     keys_copy.start()
     vals_copy.start()
-    wgu_copy.start()
     wd_copy.start()
 
     wide = ("req", "kv")
@@ -276,15 +274,11 @@
     ffn_finish()
     for k in range(narrow_n):
         ffn_rows[owned * k : owned * (k + 1), :] = y_ffn[k].astype(jnp.float32)
-    wgu_copy.wait()
     wd_copy.wait()
-    gate_up = jnp.dot(
-        ffn_rows[...].astype(jnp.bfloat16), wgu_v[...], preferred_element_type=jnp.float32
-    )
-    hidden_width = wd_v.shape[0]
-    hidden = (
-        jax.nn.gelu(gate_up[:, :hidden_width], approximate=True) * gate_up[:, hidden_width:]
-    ).astype(jnp.bfloat16)
+    ffn_x = ffn_rows[...].astype(jnp.bfloat16)
+    gate = jnp.dot(ffn_x, wgu_ref[:, 0, :], preferred_element_type=jnp.float32)
+    up = jnp.dot(ffn_x, wgu_ref[:, 1, :], preferred_element_type=jnp.float32)
+    hidden = (jax.nn.gelu(gate, approximate=True) * up).astype(jnp.bfloat16)
     ffn_out[...] = jnp.dot(hidden, wd_v[...], preferred_element_type=jnp.float32)
     for k in range(narrow_n):
         send_red[k] = ffn_out[owned * k : owned * (k + 1), :].astype(jnp.bfloat16)
@@ -320,7 +314,7 @@
     return pl.pallas_call(
         layer_kernel,
         out_shape=jax.ShapeDtypeStruct((owned, width), bf16),
-        in_specs=[vmem] * 7 + [anywhere] + [vmem] * 3 + [anywhere, anywhere],
+        in_specs=[vmem] * 7 + [anywhere] + [vmem] * 4 + [anywhere],
         out_specs=vmem,
         scratch_shapes=[
             pltpu.VMEM((n_req, per_pool, feature_width), bf16),
@@ -346,7 +340,7 @@
             pltpu.VMEM((n_narrow * owned, width), f32),
             pltpu.VMEM((n_narrow, owned, width), bf16),
             pltpu.VMEM((n_narrow, owned, width), bf16),
-            pltpu.VMEM(wgu.shape, bf16),
+            pltpu.VMEM((8, 128), bf16),
             pltpu.VMEM(wd.shape, bf16),
             dma((n_req,)), dma((n_req,)),
             dma((n_req,)), dma((n_req,)),
@@ -466,7 +460,7 @@
         unperm,
         output_weight[0],
         residual.astype(jnp.float32),
-        w_gateup.reshape(model_width, 2 * hidden_width),
+        w_gateup,
         w_down,
         0,
     )

time: 64 us -> 82.5 us (1.29)
  Pallas kernels: 50.2 us -> 60.4 us
  local copies, waits for them, and re-layouts: 9.78 us -> 15 us
  other arithmetic: 3.54 us -> 6.22 us
    pallas_call x1, Pallas kernels: 50.2 us -> 60.4 us  [layer(): pl.pallas_call(layer_kernel, out_shape=jax.ShapeDtypeStruct((owned, width...]
    convert_element_type x1, local copies, waits for them, and re-layouts: 0.08 us -> 1.44 us  [shards(): unperm = unperm.reshape(request_count, 8 * req_total).astype(jnp.bfloat16)]
    unnamed x17 -> x24, local copies, waits for them, and re-layouts: 7.21 us -> 8.53 us
    convert_element_type x1, local copies, waits for them, and re-layouts: 0.52 us -> 1.5 us  [shards(): order_pad.reshape(8 * req_total, 8 * req_total).astype(jnp.bfloat16)]
    convert_element_type x1, local copies, waits for them, and re-layouts: 0.06 us -> 0.98 us  [shards(): mask16 = jnp.tile(live, (per_group, 1)).astype(jnp.int32)]
where the time goes in v6:
time: 82.5 us; the launch traced here: 81.8 us
  Pallas kernels  60.4 us (73%)
  local copies, waits for them, and re-layouts  15 us (18%)
  other arithmetic  6.22 us (8%)
    pallas_call x1, Pallas kernels, layer(): pl.pallas_call(layer_kernel, out_shape=jax.ShapeDtypeStruct((owned, width...  60.4 us
    unnamed x24, local copies, waits for them, and re-layouts  8.53 us

profile of v6, /device:TPU:1, one launch (start us, length us, event | category | flops | bytes accessed | tf_op | source)
XLA Modules:
  0.0 81.8 jit_solution(11697954511836046012)
XLA Ops:
  0.0 0.0 copy-start
  0.0 0.0 copy-start.1
  0.0 0.9 %copy-done = s32[64,8,32]{0,2,1:T(8,128)S(1)} copy-done((s32[64,8,32]{0,2,1:T(8,128)S(1)}, s32[64,8,32]{0,2,1:T(8,128)}, u32[]{:S(2)}) %copy-start) | copy-done | bytes 65560
  0.9 0.1 and.62
  1.1 0.0 copy-start.10
  1.1 0.5 broadcast.258
  1.6 0.7 reduce.9
  2.3 0.1 div.42
  2.4 0.0 copy-start.9
  2.4 0.1 broadcast_compare_fusion
  2.5 0.9 %pad_convert_fusion = bf16[16,8,16,8]{3,2,1,0:T(8,128)(2,1)} fusion(pred[16,4,16,4]{3,2,1,0:T(8,128)(4,1)S(1)} %broadcast_compare_fusion), kind=kLoop, calls=%fused_computation | loop fusion | flops 16384 | bytes 36864 | tf_op jit(solution)/shard_map/convert_element_type | solution.py:418
  3.4 1.5 %reshape.250.order_ref = bf16[128,128]{1,0:T(8,128)(2,1)S(1)} reshape(bf16[16,8,16,8]{3,2,1,0:T(8,128)(2,1)} %pad_convert_fusion) | data formatting | bytes 65536 | tf_op jit(solution)/shard_map/convert_element_type | solution.py:418
  4.9 0.9 %copy.16 = bf16[16,8,2,256]{3,1,2,0:T(8,128)(2,1)S(1)} copy(bf16[16,8,2,256]{3,2,1,0:T(2,128)(2,1)} %bitcast.29) | data formatting | bytes 262144
  5.9 0.0 copy-done.9
  5.9 1.0 %pad_maximum_fusion.projw_ref = bf16[128,1536]{1,0:T(8,128)(2,1)S(1)} fusion(bf16[128,512]{1,0:T(8,128)(2,1)S(1)} %bitcast.28, bf16[128,1024]{1,0:T(8,128)(2,1)} %param.14), kind=kLoop, calls=%fused_computation.1 | loop fusion | flops 786432 | bytes 786432 | tf_op jit(solution)/shard_map/concatenate | solution.py:423
  6.9 0.7 fusion.7
  7.6 0.1 select_reduce_fusion.2
  7.7 0.1 multiply_cosine_fusion
  7.8 0.6 pad_maximum_fusion.1.trig_ref
  8.4 0.0 copy-done.10
  8.4 0.1 select_reduce_fusion.1
  8.6 0.1 fusion
  8.7 0.1 and.68
  8.8 0.1 and.69
  8.9 0.1 select_reduce_fusion
  9.0 0.1 broadcast_reduce_fusion
  9.1 0.1 add.88
  9.2 0.1 add.90
  9.3 0.1 compare_and_fusion
  9.4 0.7 tile.2
  10.1 1.0 %convert_element_type.37.mask_ref = s32[16,2816]{1,0:T(8,128)S(1)} reshape(s32[4,4,2816]{2,1,0:T(4,128)} %tile.2) | data formatting | bytes 360448 | tf_op jit(solution)/shard_map/convert_element_type | solution.py:447
  11.1 0.8 broadcast_compare_fusion.1
  11.9 0.6 fusion.1
  12.5 1.4 %copy.15.unperm_ref = bf16[64,128]{1,0:T(8,128)(2,1)} copy(bf16[64,128]{0,1:T(8,128)(2,1)} %fusion.1) | data formatting | bytes 32768 | tf_op jit(solution)/shard_map/convert_element_type | solution.py:421
  13.9 0.7 bitcast_convert_fusion.resid_ref
  14.7 0.0 copy-done.1
  14.7 0.0 copy-start.2
  14.7 1.6 %copy-done.2 = bf16[512,2048]{1,0:T(8,128)(2,1)S(1)} copy-done((bf16[512,2048]{1,0:T(8,128)(2,1)S(1)}, bf16[512,2048]{1,0:T(8,128)(2,1)}, u32[]{:S(2)}) %copy-start.2) | copy-done | bytes 2097176
  16.3 0.0 copy-start.3
  16.3 0.9 %copy-done.3 = bf16[1,64,2048]{2,1,0:T(8,128)(2,1)S(1)} copy-done((bf16[1,64,2048]{2,1,0:T(8,128)(2,1)S(1)}, bf16[1,64,2048]{2,1,0:T(8,128)(2,1)}, u32[]{:S(2)}) %copy-start.3) | copy-done | bytes 262168
  17.2 0.0 copy-start.4
  17.2 0.7 copy-done.4
  17.9 0.7 copy-done.5
  18.7 0.8 copy-done.6
  19.4 0.7 copy-done.7
  20.1 0.7 copy-done.8
  20.8 60.4 %shard_map.109 = bf16[2,2048]{1,0:T(2,128)(2,1)S(1)} custom-call(bf16[4,2048]{1,0:T(4,128)(2,1)S(1)} %bitcast.26, f32[4,2048]{1,0:T(4,128)S(1)} %copy-done.6, f32[2,256]{1,0:T(2,128)S(1)} %copy-done.8, bf16[128,128]{1,0:T(8,128)(2,1)S(1)} %reshape.250.order_ref, bf16[128,1536]{1,0:T(8,128)(2,1)S(1)} %pad_maximum_fusion.projw_ref, ...), custom_call_target="tpu_custom_call" | custom-call | tf_op jit(solution)/shard_map/pallas_call | solution.py:314
  81.2 0.6 copy.18
  (15 shorter events, 0.1 us)
Async XLA Ops:
  0.0 0.9 %copy-start = (s32[64,8,32]{0,2,1:T(8,128)S(1)}, s32[64,8,32]{0,2,1:T(8,128)}, u32[]{:S(2)}) copy-start(s32[64,8,32]{0,2,1:T(8,128)} %param.21) | copy-start | bytes 196612
  0.0 14.7 %copy-start.1 = (bf16[43,2,64,256]{3,2,1,0:T(8,128)(2,1)S(1)}, bf16[43,2,64,256]{3,2,1,0:T(8,128)(2,1)}, u32[]{:S(2)}) copy-start(bf16[43,2,64,256]{3,2,1,0:T(8,128)(2,1)} %kv_hbm.1) | copy-start | bytes 8454148
  1.1 7.4 %copy-start.10 = (s32[64]{0:T(128)}, s32[64]{0:T(128)S(1)}, u32[]{:S(2)}) copy-start(s32[64]{0:T(128)S(1)} %get-tuple-element.7) | copy-start | bytes 772
  2.4 3.5 %copy-start.9 = (s32[16,4]{1,0:T(8,128)}, s32[16,4]{1,0:T(8,128)S(1)}, u32[]{:S(2)}) copy-start(s32[16,4]{1,0:T(8,128)S(1)} %get-tuple-element.12) | copy-start | bytes 772
  14.7 1.6 %copy-start.2 = (bf16[512,2048]{1,0:T(8,128)(2,1)S(1)}, bf16[512,2048]{1,0:T(8,128)(2,1)}, u32[]{:S(2)}) copy-start(bf16[512,2048]{1,0:T(8,128)(2,1)} %wd_hbm.1) | copy-start | bytes 6291460
  16.3 0.9 %copy-start.3 = (bf16[1,64,2048]{2,1,0:T(8,128)(2,1)S(1)}, bf16[1,64,2048]{2,1,0:T(8,128)(2,1)}, u32[]{:S(2)}) copy-start(bf16[1,64,2048]{2,1,0:T(8,128)(2,1)} %param.16) | copy-start | bytes 786436
  17.2 0.7 copy-start.4
  17.9 0.7 copy-start.5
  18.7 0.8 copy-start.6
  19.4 0.7 copy-start.7
  20.1 0.7 copy-start.8

commit v7 on v5

--- a/solution.py
+++ b/solution.py
@@ -127,20 +127,27 @@
     return value_entries * lax.rsqrt(mean_square + eps_norm) * gain_row
 
 
+def unpack_rows(wgu_raw, wgu_v, start, count):
+    hidden_width = wgu_raw.shape[2]
+    rows = pl.ds(start, count)
+    wgu_v[rows, 0:hidden_width] = wgu_raw[rows, 0, :]
+    wgu_v[rows, hidden_width:] = wgu_raw[rows, 1, :]
+
+
 def layer_kernel(
     tok_ref, gains_ref, qkg_ref, order_ref, projw_ref, trig_ref, mask_ref, kv_hbm,
     unperm_ref, wout_ref, resid_ref, wgu_hbm, wd_hbm,
     out_ref,
     tok_src, y_tok, tok_rows, send_qkv, y_qkv, keys_v, vals_v, q16, k16, v16, comb,
     send_att, y_att, att_rows, w_pad, send_proj, y_proj, ffn_src, y_ffn, ffn_rows, ffn_out,
-    send_red, y_red, wgu_v, wd_v,
+    send_red, y_red, wgu_v, wd_v, wgu_raw,
     tok_send, tok_recv, qkv_send, qkv_recv,
     att_send, att_recv, proj_send, proj_recv, ffn_send, ffn_recv, red_send, red_recv, w_sem,
 ):
     n_pages = kv_hbm.shape[0]
     keys_copy = pltpu.make_async_copy(kv_hbm.at[:, 0], keys_v.at[pl.ds(0, n_pages)], w_sem.at[0])
     vals_copy = pltpu.make_async_copy(kv_hbm.at[:, 1], vals_v.at[pl.ds(0, n_pages)], w_sem.at[1])
-    wgu_copy = pltpu.make_async_copy(wgu_hbm, wgu_v, w_sem.at[2])
+    wgu_copy = pltpu.make_async_copy(wgu_hbm, wgu_raw, w_sem.at[2])
     wd_copy = pltpu.make_async_copy(wd_hbm, wd_v, w_sem.at[3])
     keys_copy.start()
     vals_copy.start()
@@ -175,6 +182,8 @@
 
     tok_me, tok_finish = start_copies(("req",), lambda k: tok_src.at[k], y_tok, tok_send, tok_recv)
     y_tok[tok_me] = tok_src[tok_me]
+    wgu_copy.wait()
+    unpack_rows(wgu_raw, wgu_v, 0, 512)
     tok_finish()
     for k in range(n_req):
         tok_rows[8 * k : 8 * k + per_pool, :] = y_tok[k].astype(jnp.float32)
@@ -187,6 +196,7 @@
 
     qkv_me, qkv_finish = start_copies(("req",), lambda k: send_qkv.at[k], y_qkv, qkv_send, qkv_recv)
     y_qkv[qkv_me] = send_qkv[qkv_me]
+    unpack_rows(wgu_raw, wgu_v, 512, 512)
     qkv_finish()
     summed = y_qkv[0]
     for k in range(1, n_req):
@@ -251,6 +261,7 @@
     w_pad[...] = jnp.zeros_like(w_pad)
     rows_w = wout_ref.shape[0]
     w_pad[0:rows_w, :] = wout_ref[...]
+    unpack_rows(wgu_raw, wgu_v, 1024, 512)
     att_finish()
     for k in range(n_req):
         att_rows[8 * k : 8 * k + per_pool, 0:slice_width] = y_att[k].astype(jnp.float32)
@@ -264,6 +275,7 @@
 
     proj_me, proj_finish = start_copies(wide, lambda k: send_proj.at[k], y_proj, proj_send, proj_recv)
     y_proj[proj_me] = send_proj[proj_me]
+    unpack_rows(wgu_raw, wgu_v, 1536, 512)
     proj_finish()
     projected = y_proj[0].astype(jnp.float32)
     for k in range(1, n_wide):
@@ -276,7 +288,6 @@
     ffn_finish()
     for k in range(narrow_n):
         ffn_rows[owned * k : owned * (k + 1), :] = y_ffn[k].astype(jnp.float32)
-    wgu_copy.wait()
     wd_copy.wait()
     gate_up = jnp.dot(
         ffn_rows[...].astype(jnp.bfloat16), wgu_v[...], preferred_element_type=jnp.float32
@@ -346,8 +357,9 @@
             pltpu.VMEM((n_narrow * owned, width), f32),
             pltpu.VMEM((n_narrow, owned, width), bf16),
             pltpu.VMEM((n_narrow, owned, width), bf16),
+            pltpu.VMEM((wgu.shape[0], wgu.shape[1] * wgu.shape[2]), bf16),
+            pltpu.VMEM(wd.shape, bf16),
             pltpu.VMEM(wgu.shape, bf16),
-            pltpu.VMEM(wd.shape, bf16),
             dma((n_req,)), dma((n_req,)),
             dma((n_req,)), dma((n_req,)),
             dma((n_req,)), dma((n_req,)),
@@ -466,7 +478,7 @@
         unperm,
         output_weight[0],
         residual.astype(jnp.float32),
-        w_gateup.reshape(model_width, 2 * hidden_width),
+        w_gateup,
         w_down,
         0,
     )

time: 64 us -> 72.2 us (1.13)
  local copies, waits for them, and re-layouts: 9.78 us -> 15 us
  other arithmetic: 3.54 us -> 6.22 us
    convert_element_type x1, local copies, waits for them, and re-layouts: 0.08 us -> 1.44 us  [shards(): unperm = unperm.reshape(request_count, 8 * req_total).astype(jnp.bfloat16)]
    unnamed x17 -> x24, local copies, waits for them, and re-layouts: 7.21 us -> 8.53 us
    convert_element_type x1, local copies, waits for them, and re-layouts: 0.52 us -> 1.5 us  [shards(): order_pad.reshape(8 * req_total, 8 * req_total).astype(jnp.bfloat16)]
    convert_element_type x1, local copies, waits for them, and re-layouts: 0.06 us -> 0.98 us  [shards(): mask16 = jnp.tile(live, (per_group, 1)).astype(jnp.int32)]
    convert_element_type x1, other arithmetic: 0.12 us -> 0.92 us  [shards(): order_pad.reshape(8 * req_total, 8 * req_total).astype(jnp.bfloat16)]
where the time goes in v7:
time: 72.2 us; the launch traced here: 71.4 us
  Pallas kernels  50.1 us (69%)
  local copies, waits for them, and re-layouts  15 us (21%)
  other arithmetic  6.22 us (9%)
    pallas_call x1, Pallas kernels, layer(): pl.pallas_call(layer_kernel, out_shape=jax.ShapeDtypeStruct((owned, width...  50.1 us
    unnamed x24, local copies, waits for them, and re-layouts  8.53 us
    convert_element_type x1, local copies, waits for them, and re-layouts, shards(): order_pad.reshape(8 * req_total, 8 * req_total).astype(jnp.bfloat16)  1.5 us

profile of v7, /device:TPU:1, one launch (start us, length us, event | category | flops | bytes accessed | tf_op | source)
XLA Modules:
  0.0 71.4 jit_solution(17471749217115003702)
XLA Ops:
  0.0 0.0 copy-start
  0.0 0.0 copy-start.1
  0.0 0.9 %copy-done = s32[64,8,32]{0,2,1:T(8,128)S(1)} copy-done((s32[64,8,32]{0,2,1:T(8,128)S(1)}, s32[64,8,32]{0,2,1:T(8,128)}, u32[]{:S(2)}) %copy-start) | copy-done | bytes 65560
  0.9 0.1 and.62
  1.1 0.0 copy-start.10
  1.1 0.5 broadcast.258
  1.6 0.7 reduce.9
  2.3 0.1 div.42
  2.4 0.0 copy-start.9
  2.4 0.1 broadcast_compare_fusion
  2.5 0.9 %pad_convert_fusion = bf16[16,8,16,8]{3,2,1,0:T(8,128)(2,1)} fusion(pred[16,4,16,4]{3,2,1,0:T(8,128)(4,1)S(1)} %broadcast_compare_fusion), kind=kLoop, calls=%fused_computation | loop fusion | flops 16384 | bytes 36864 | tf_op jit(solution)/shard_map/convert_element_type | solution.py:436
  3.4 1.5 %reshape.250.order_ref = bf16[128,128]{1,0:T(8,128)(2,1)S(1)} reshape(bf16[16,8,16,8]{3,2,1,0:T(8,128)(2,1)} %pad_convert_fusion) | data formatting | bytes 65536 | tf_op jit(solution)/shard_map/convert_element_type | solution.py:436
  4.9 0.9 %copy.16 = bf16[16,8,2,256]{3,1,2,0:T(8,128)(2,1)S(1)} copy(bf16[16,8,2,256]{3,2,1,0:T(2,128)(2,1)} %bitcast.29) | data formatting | bytes 262144
  5.9 0.0 copy-done.9
  5.9 1.0 %pad_maximum_fusion.projw_ref = bf16[128,1536]{1,0:T(8,128)(2,1)S(1)} fusion(bf16[128,512]{1,0:T(8,128)(2,1)S(1)} %bitcast.28, bf16[128,1024]{1,0:T(8,128)(2,1)} %param.14), kind=kLoop, calls=%fused_computation.1 | loop fusion | flops 786432 | bytes 786432 | tf_op jit(solution)/shard_map/concatenate | solution.py:441
  6.9 0.7 fusion.7
  7.6 0.1 select_reduce_fusion.2
  7.7 0.1 multiply_cosine_fusion
  7.8 0.6 pad_maximum_fusion.1.trig_ref
  8.4 0.0 copy-done.10
  8.4 0.1 select_reduce_fusion.1
  8.6 0.1 fusion
  8.7 0.1 and.68
  8.8 0.1 and.69
  8.9 0.1 select_reduce_fusion
  9.0 0.1 broadcast_reduce_fusion
  9.1 0.1 add.88
  9.2 0.1 add.90
  9.3 0.1 compare_and_fusion
  9.4 0.7 tile.2
  10.1 1.0 %convert_element_type.37.mask_ref = s32[16,2816]{1,0:T(8,128)S(1)} reshape(s32[4,4,2816]{2,1,0:T(4,128)} %tile.2) | data formatting | bytes 360448 | tf_op jit(solution)/shard_map/convert_element_type | solution.py:465
  11.1 0.8 %broadcast_compare_fusion.1 = pred[64,16,4]{0,2,1:T(4,128)(4,1)S(1)} fusion(s32[16,4]{1,0:T(8,128)} %copy-done.9, s32[64]{0:T(128)} %copy-done.10), kind=kLoop, calls=%fused_computation.11 | loop fusion | flops 4096 | bytes 4608 | tf_op jit(solution)/shard_map/eq | solution.py:432
  11.9 0.6 fusion.1
  12.5 1.4 %copy.15.unperm_ref = bf16[64,128]{1,0:T(8,128)(2,1)} copy(bf16[64,128]{0,1:T(8,128)(2,1)} %fusion.1) | data formatting | bytes 32768 | tf_op jit(solution)/shard_map/convert_element_type | solution.py:439
  13.9 0.7 %bitcast_convert_fusion.resid_ref = f32[2,2048]{1,0:T(2,128)S(1)} fusion(bf16[4,1,2048]{2,0,1:T(4,128)(2,1)} %param.11, s32[]{:T(128)S(6)} %select_n.71), kind=kLoop, calls=%fused_computation.23 | loop fusion | flops 4096 | bytes 24580 | tf_op jit(solution)/shard_map/convert_element_type | solution.py:480
  14.7 0.0 copy-done.1
  14.7 0.0 copy-start.2
  14.7 1.6 %copy-done.2 = bf16[512,2048]{1,0:T(8,128)(2,1)S(1)} copy-done((bf16[512,2048]{1,0:T(8,128)(2,1)S(1)}, bf16[512,2048]{1,0:T(8,128)(2,1)}, u32[]{:S(2)}) %copy-start.2) | copy-done | bytes 2097176
  16.3 0.0 copy-start.3
  16.3 0.9 %copy-done.3 = bf16[1,64,2048]{2,1,0:T(8,128)(2,1)S(1)} copy-done((bf16[1,64,2048]{2,1,0:T(8,128)(2,1)S(1)}, bf16[1,64,2048]{2,1,0:T(8,128)(2,1)}, u32[]{:S(2)}) %copy-start.3) | copy-done | bytes 262168
  17.2 0.0 copy-start.4
  17.2 0.7 %copy-done.4 = bf16[64,128]{1,0:T(8,128)(2,1)S(1)} copy-done((bf16[64,128]{1,0:T(8,128)(2,1)S(1)}, bf16[64,128]{1,0:T(8,128)(2,1)}, u32[]{:S(2)}) %copy-start.4) | copy-done | bytes 16408
  17.9 0.7 %copy-done.5 = bf16[4,1,2048]{2,0,1:T(4,128)(2,1)S(1)} copy-done((bf16[4,1,2048]{2,0,1:T(4,128)(2,1)S(1)}, bf16[4,1,2048]{2,0,1:T(4,128)(2,1)}, u32[]{:S(2)}) %copy-start.5) | copy-done | bytes 16408
  18.7 0.8 %copy-done.6 = f32[4,2048]{1,0:T(4,128)S(1)} copy-done((f32[4,2048]{1,0:T(4,128)S(1)}, f32[4,2048]{1,0:T(4,128)}, u32[]{:S(2)}) %copy-start.6) | copy-done | bytes 32792
  19.4 0.7 copy-done.7
  20.1 0.7 copy-done.8
  20.8 50.1 %shard_map.109 = bf16[2,2048]{1,0:T(2,128)(2,1)S(1)} custom-call(bf16[4,2048]{1,0:T(4,128)(2,1)S(1)} %bitcast.26, f32[4,2048]{1,0:T(4,128)S(1)} %copy-done.6, f32[2,256]{1,0:T(2,128)S(1)} %copy-done.8, bf16[128,128]{1,0:T(8,128)(2,1)S(1)} %reshape.250.order_ref, bf16[128,1536]{1,0:T(8,128)(2,1)S(1)} %pad_maximum_fusion.projw_ref, ...), custom_call_target="tpu_custom_call" | custom-call | tf_op jit(solution)/shard_map/pallas_call | solution.py:331
  70.8 0.6 copy.18
  (15 shorter events, 0.1 us)
Async XLA Ops:
  0.0 0.9 %copy-start = (s32[64,8,32]{0,2,1:T(8,128)S(1)}, s32[64,8,32]{0,2,1:T(8,128)}, u32[]{:S(2)}) copy-start(s32[64,8,32]{0,2,1:T(8,128)} %param.21) | copy-start | bytes 196612
  0.0 14.7 %copy-start.1 = (bf16[43,2,64,256]{3,2,1,0:T(8,128)(2,1)S(1)}, bf16[43,2,64,256]{3,2,1,0:T(8,128)(2,1)}, u32[]{:S(2)}) copy-start(bf16[43,2,64,256]{3,2,1,0:T(8,128)(2,1)} %kv_hbm.1) | copy-start | bytes 8454148
  1.1 7.4 %copy-start.10 = (s32[64]{0:T(128)}, s32[64]{0:T(128)S(1)}, u32[]{:S(2)}) copy-start(s32[64]{0:T(128)S(1)} %get-tuple-element.7) | copy-start | bytes 772
  2.4 3.5 %copy-start.9 = (s32[16,4]{1,0:T(8,128)}, s32[16,4]{1,0:T(8,128)S(1)}, u32[]{:S(2)}) copy-start(s32[16,4]{1,0:T(8,128)S(1)} %get-tuple-element.12) | copy-start | bytes 772
  14.7 1.6 %copy-start.2 = (bf16[512,2048]{1,0:T(8,128)(2,1)S(1)}, bf16[512,2048]{1,0:T(8,128)(2,1)}, u32[]{:S(2)}) copy-start(bf16[512,2048]{1,0:T(8,128)(2,1)} %wd_hbm.1) | copy-start | bytes 6291460
  16.3 0.9 %copy-start.3 = (bf16[1,64,2048]{2,1,0:T(8,128)(2,1)S(1)}, bf16[1,64,2048]{2,1,0:T(8,128)(2,1)}, u32[]{:S(2)}) copy-start(bf16[1,64,2048]{2,1,0:T(8,128)(2,1)} %param.16) | copy-start | bytes 786436
  17.2 0.7 %copy-start.4 = (bf16[64,128]{1,0:T(8,128)(2,1)S(1)}, bf16[64,128]{1,0:T(8,128)(2,1)}, u32[]{:S(2)}) copy-start(bf16[64,128]{1,0:T(8,128)(2,1)} %copy.15.unperm_ref) | copy-start | bytes 49156
  17.9 0.7 %copy-start.5 = (bf16[4,1,2048]{2,0,1:T(4,128)(2,1)S(1)}, bf16[4,1,2048]{2,0,1:T(4,128)(2,1)}, u32[]{:S(2)}) copy-start(bf16[4,1,2048]{2,0,1:T(4,128)(2,1)} %param.11) | copy-start | bytes 49156
  18.7 0.8 %copy-start.6 = (f32[4,2048]{1,0:T(4,128)S(1)}, f32[4,2048]{1,0:T(4,128)}, u32[]{:S(2)}) copy-start(f32[4,2048]{1,0:T(4,128)} %gains_ref.1) | copy-start | bytes 98308
  19.4 0.7 copy-start.7
  20.1 0.7 copy-start.8

commit v8 on v7

--- a/solution.py
+++ b/solution.py
@@ -369,7 +369,7 @@
             dma((4,)),
         ],
         compiler_params=pltpu.CompilerParams(
-            collective_id=cid, has_side_effects=True, vmem_limit_bytes=48 * 1024 * 1024
+            collective_id=cid, has_side_effects=True
         ),
     )(tok, gains, qk_gains, order_pad, projw, trig, mask16, kv_cache,
       unperm, wout, residual, wgu, wd)

time: 72.2 us -> 63.9 us (0.89)
  local copies, waits for them, and re-layouts: 15 us -> 7.57 us
  other arithmetic: 6.22 us -> 4.74 us
  Pallas kernels: 50.1 us -> 51.2 us
    unnamed x24 -> x6, local copies, waits for them, and re-layouts: 8.53 us -> 3.13 us
    pallas_call x1, Pallas kernels: 50.1 us -> 51.2 us  [layer(): pl.pallas_call(layer_kernel, out_shape=jax.ShapeDtypeStruct((owned, width...]
    convert_element_type x1, other arithmetic: 0.92 us -> 0.12 us  [shards(): order_pad.reshape(8 * req_total, 8 * req_total).astype(jnp.bfloat16)]
    convert_element_type x1, local copies, waits for them, and re-layouts: 1.44 us -> 0.69 us  [shards(): unperm = unperm.reshape(request_count, 8 * req_total).astype(jnp.bfloat16)]
    concatenate x1, other arithmetic: 0.98 us -> 1.71 us  [shards(): jnp.concatenate([w_query, key_value_weight.reshape(key_value_weight.shape...]
where the time goes in v8:
time: 63.9 us; the launch traced here: 63.6 us
  Pallas kernels  51.2 us (80%)
  local copies, waits for them, and re-layouts  7.57 us (12%)
  other arithmetic  4.74 us (7%)
    pallas_call x1, Pallas kernels, layer(): pl.pallas_call(layer_kernel, out_shape=jax.ShapeDtypeStruct((owned, width...  51.2 us
    unnamed x6, local copies, waits for them, and re-layouts  3.13 us
    concatenate x1, other arithmetic, shards(): jnp.concatenate([w_query, key_value_weight.reshape(key_value_weight.shape...  1.71 us

profile of v8, /device:TPU:1, one launch (start us, length us, event | category | flops | bytes accessed | tf_op | source)
XLA Modules:
  0.0 63.6 jit_solution(15545561156704572505)
XLA Ops:
  0.0 0.0 copy-start
  0.0 0.0 copy-start.1
  0.0 0.9 %copy-done = s32[64,8,32]{0,2,1:T(8,128)S(1)} copy-done((s32[64,8,32]{0,2,1:T(8,128)S(1)}, s32[64,8,32]{0,2,1:T(8,128)}, u32[]{:S(2)}) %copy-start) | copy-done | bytes 65560
  0.9 0.1 and.62
  1.1 0.5 broadcast.258
  1.6 0.7 %reduce.9 = s32[64]{0:T(128)S(1)} reduce(s32[64,1]{0,1:T(1,128)S(1)} %get-tuple-element.8, s32[]{:T(128)} %broadcast.258), dimensions={1}, to_apply=%slice_divide_fusion.reduce_sub_computation | reduce | bytes 516 | tf_op jit(solution)/shard_map/jit(floor_divide)/div | solution.py:430
  2.2 0.1 div.42
  2.4 0.1 broadcast_compare_fusion
  2.5 0.1 pad_convert_fusion
  2.6 1.1 %reshape.250.order_ref = bf16[128,128]{1,0:T(8,128)(2,1)} reshape(bf16[16,8,16,8]{3,2,1,0:T(8,128)(2,1)S(1)} %pad_convert_fusion) | data formatting | bytes 65536 | tf_op jit(solution)/shard_map/convert_element_type | solution.py:436
  3.8 0.9 %copy.16 = bf16[16,8,2,256]{3,1,2,0:T(8,128)(2,1)S(1)} copy(bf16[16,8,2,256]{3,2,1,0:T(2,128)(2,1)} %bitcast.27) | data formatting | bytes 262144
  4.7 1.7 %pad_maximum_fusion.projw_ref = bf16[128,1536]{1,0:T(8,128)(2,1)} fusion(bf16[128,512]{1,0:T(8,128)(2,1)S(1)} %bitcast.25, bf16[128,1024]{1,0:T(8,128)(2,1)} %param.14), kind=kLoop, calls=%fused_computation.1 | loop fusion | flops 786432 | bytes 786432 | tf_op jit(solution)/shard_map/concatenate | solution.py:441
  6.4 0.7 %fusion.7 = s32[64]{0:T(128)S(1)} fusion(s32[64,8]{0,1:T(8,128)} %param.20, s32[]{:T(128)S(6)} %select_n.60), kind=kLoop, calls=%fused_computation.42 | loop fusion | bytes 516 | tf_op jit(solution)/shard_map/jit(_where)/broadcast_in_dim | solution.py:446
  7.1 0.1 select_reduce_fusion.2
  7.2 0.1 multiply_cosine_fusion
  7.3 0.6 pad_maximum_fusion.1.trig_ref
  8.0 0.1 select_reduce_fusion.1
  8.1 0.1 fusion
  8.2 0.1 and.68
  8.3 0.1 and.69
  8.4 0.1 select_reduce_fusion
  8.5 0.1 broadcast_reduce_fusion
  8.7 0.1 add.88
  8.7 0.1 add.90
  8.8 0.1 compare_and_fusion
  9.0 0.7 %convert_element_type.37.mask_ref = s32[16,2816]{1,0:T(8,128)} reshape(s32[4,4,2816]{2,1,0:T(4,128)S(1)} %tile.2) | data formatting | bytes 360448 | tf_op jit(solution)/shard_map/convert_element_type | solution.py:465
  9.7 0.1 broadcast_compare_fusion.1
  9.8 0.7 %copy.15.unperm_ref = bf16[64,128]{1,0:T(8,128)(2,1)} copy(bf16[64,128]{0,1:T(8,128)(2,1)S(1)} %fusion.1) | data formatting | bytes 32768 | tf_op jit(solution)/shard_map/convert_element_type | solution.py:439
  10.5 0.0 copy-done.1
  10.5 0.6 bitcast_convert_fusion.resid_ref
  11.1 51.2 %shard_map.109 = bf16[2,2048]{1,0:T(2,128)(2,1)} custom-call(bf16[4,2048]{1,0:T(4,128)(2,1)} %bitcast.28, f32[4,2048]{1,0:T(4,128)} %gains_ref.1, f32[2,256]{1,0:T(2,128)} %qkg_ref.1, bf16[128,128]{1,0:T(8,128)(2,1)} %reshape.250.order_ref, bf16[128,1536]{1,0:T(8,128)(2,1)} %pad_maximum_fusion.projw_ref, f32[2,4,128]{2,1,0:T(4,128)} %pad_maximum_fusion.1.trig_ref, ...), custom_call_target="tpu_custom_call" | custom-call | tf_op jit(solution)/shard_map/pallas_call | solution.py:331
  62.3 1.3 %copy.18 = bf16[2,1,2048]{2,0,1:T(2,128)(2,1)} copy(bf16[2,1,2048]{2,0,1:T(2,128)(2,1)} %bitcast.29) | data formatting | bytes 16384
  (13 shorter events, 0.2 us)
Async XLA Ops:
  0.0 0.9 %copy-start = (s32[64,8,32]{0,2,1:T(8,128)S(1)}, s32[64,8,32]{0,2,1:T(8,128)}, u32[]{:S(2)}) copy-start(s32[64,8,32]{0,2,1:T(8,128)} %param.21) | copy-start | bytes 196612
  0.0 10.5 %copy-start.1 = (bf16[4,1,2048]{2,0,1:T(4,128)(2,1)S(1)}, bf16[4,1,2048]{2,0,1:T(4,128)(2,1)}, u32[]{:S(2)}) copy-start(bf16[4,1,2048]{2,0,1:T(4,128)(2,1)} %param.11) | copy-start | bytes 49156

commit v9 on v8

--- a/solution.py
+++ b/solution.py
@@ -135,12 +135,12 @@
 
 
 def layer_kernel(
-    tok_ref, gains_ref, qkg_ref, order_ref, projw_ref, trig_ref, mask_ref, kv_hbm,
-    unperm_ref, wout_ref, resid_ref, wgu_hbm, wd_hbm,
+    tok_ref, gains_ref, qkg_ref, order_ref, wq_ref, kvw_ref, trig_ref, mask_ref, kv_hbm,
+    unperm_ref, wout_ref, wgu_hbm, wd_hbm,
     out_ref,
     tok_src, y_tok, tok_rows, send_qkv, y_qkv, keys_v, vals_v, q16, k16, v16, comb,
     send_att, y_att, att_rows, w_pad, send_proj, y_proj, ffn_src, y_ffn, ffn_rows, ffn_out,
-    send_red, y_red, wgu_v, wd_v, wgu_raw,
+    send_red, y_red, wgu_v, wd_v, wgu_raw, kv_v,
     tok_send, tok_recv, qkv_send, qkv_recv,
     att_send, att_recv, proj_send, proj_recv, ffn_send, ffn_recv, red_send, red_recv, w_sem,
 ):
@@ -178,6 +178,9 @@
     for k in range(n_req):
         tok_src[k] = normed[:, feature_width * k : feature_width * (k + 1)]
     tok_rows[...] = jnp.zeros_like(tok_rows)
+    kv_half = kvw_ref.shape[2]
+    kv_v[:, 0:kv_half] = kvw_ref[:, 0, :]
+    kv_v[:, kv_half:] = kvw_ref[:, 1, :]
     pl.semaphore_wait(barrier, wide_n - 1 + narrow_n - 2)
 
     tok_me, tok_finish = start_copies(("req",), lambda k: tok_src.at[k], y_tok, tok_send, tok_recv)
@@ -190,9 +193,12 @@
     pooled = jnp.dot(
         order_ref[...], tok_rows[...].astype(jnp.bfloat16), preferred_element_type=jnp.float32
     ).astype(jnp.bfloat16)
-    partial = jnp.dot(pooled, projw_ref[...], preferred_element_type=jnp.float32)
+    q_width = wq_ref.shape[1]
+    partial_q = jnp.dot(pooled, wq_ref[...], preferred_element_type=jnp.float32)
+    partial_kv = jnp.dot(pooled, kv_v[...], preferred_element_type=jnp.float32)
     for k in range(n_req):
-        send_qkv[k] = partial[8 * k : 8 * k + per_pool]
+        send_qkv[k, :, 0:q_width] = partial_q[8 * k : 8 * k + per_pool]
+        send_qkv[k, :, q_width:] = partial_kv[8 * k : 8 * k + per_pool]
 
     qkv_me, qkv_finish = start_copies(("req",), lambda k: send_qkv.at[k], y_qkv, qkv_send, qkv_recv)
     y_qkv[qkv_me] = send_qkv[qkv_me]
@@ -280,7 +286,9 @@
     projected = y_proj[0].astype(jnp.float32)
     for k in range(1, n_wide):
         projected = projected + y_proj[k].astype(jnp.float32)
-    middle = (resid_ref[...] + rms_rows(projected, gains_ref[1:2, :])).astype(jnp.bfloat16)
+    own = tok_ref[...].astype(jnp.float32)
+    residual = jnp.where(lax.axis_index("kv") == 0, own[0:owned], own[owned : 2 * owned])
+    middle = (residual + rms_rows(projected, gains_ref[1:2, :])).astype(jnp.bfloat16)
     ffn_src[...] = rms_rows(middle.astype(jnp.float32), gains_ref[2:3, :]).astype(jnp.bfloat16)
 
     ffn_me, ffn_finish = start_copies(narrow, lambda k: ffn_src, y_ffn, ffn_send, ffn_recv)
@@ -311,15 +319,15 @@
     )
 
 
-def layer(tok, gains, qk_gains, order_pad, projw, trig, mask16, kv_cache,
-          unperm, wout, residual, wgu, wd, cid):
+def layer(tok, gains, qk_gains, order_pad, wq, kvw, trig, mask16, kv_cache,
+          unperm, wout, wgu, wd, cid):
     n_req = lax.axis_size("req")
     n_wide = n_req * lax.axis_size("kv")
     n_narrow = lax.axis_size("kv") * lax.axis_size("hid")
-    owned, width = residual.shape
-    per_pool = tok.shape[0]
+    per_pool, width = tok.shape
+    owned = per_pool // lax.axis_size("kv")
     feature_width = width // n_req
-    qkv_width = projw.shape[1]
+    qkv_width = wq.shape[1] + kvw.shape[1] * kvw.shape[2]
     n_pages, _, page_size, head_width = kv_cache.shape
     slice_width = wout.shape[0]
     rows16 = mask16.shape[0]
@@ -331,7 +339,7 @@
     return pl.pallas_call(
         layer_kernel,
         out_shape=jax.ShapeDtypeStruct((owned, width), bf16),
-        in_specs=[vmem] * 7 + [anywhere] + [vmem] * 3 + [anywhere, anywhere],
+        in_specs=[vmem] * 8 + [anywhere] + [vmem] * 2 + [anywhere, anywhere],
         out_specs=vmem,
         scratch_shapes=[
             pltpu.VMEM((n_req, per_pool, feature_width), bf16),
@@ -360,6 +368,7 @@
             pltpu.VMEM((wgu.shape[0], wgu.shape[1] * wgu.shape[2]), bf16),
             pltpu.VMEM(wd.shape, bf16),
             pltpu.VMEM(wgu.shape, bf16),
+            pltpu.VMEM((kvw.shape[0], kvw.shape[1] * kvw.shape[2]), bf16),
             dma((n_req,)), dma((n_req,)),
             dma((n_req,)), dma((n_req,)),
             dma((n_req,)), dma((n_req,)),
@@ -371,8 +380,8 @@
         compiler_params=pltpu.CompilerParams(
             collective_id=cid, has_side_effects=True
         ),
-    )(tok, gains, qk_gains, order_pad, projw, trig, mask16, kv_cache,
-      unperm, wout, residual, wgu, wd)
+    )(tok, gains, qk_gains, order_pad, wq, kvw, trig, mask16, kv_cache,
+      unperm, wout, wgu, wd)
 
 def rms_scale(value_entries, gain_row):
     mean_square = jnp.mean(value_entries * value_entries, axis=-1, keepdims=True)
@@ -438,9 +447,6 @@
     unperm = jnp.pad(unperm, ((0, 0), (0, 0), (0, pad_to)))
     unperm = unperm.reshape(request_count, 8 * req_total).astype(jnp.bfloat16)
 
-    projection = jnp.concatenate(
-        [w_query, key_value_weight.reshape(key_value_weight.shape[0], -1)], axis=1
-    )
 
     mine = lax.dynamic_slice_in_dim(order, req_position * rows_here, rows_here, 0)
     my_lengths = jnp.sum(jnp.where(mine, group_lengths[None, :], 0), axis=1)
@@ -464,20 +470,19 @@
     live = jnp.pad(live, ((0, 0), (0, page_size)))
     mask16 = jnp.tile(live, (per_group, 1)).astype(jnp.int32)
 
-    residual = lax.dynamic_slice_in_dim(own_rows, kv_position * half_rows, half_rows, 0)
     hidden_width = w_down.shape[0]
     result = layer(
         own_rows,
         gains,
         qk_gains,
         order_pad,
-        projection,
+        w_query,
+        key_value_weight,
         trig,
         mask16,
         kv_cache,
         unperm,
         output_weight[0],
-        residual.astype(jnp.float32),
         w_gateup,
         w_down,
         0,

time: 63.9 us -> 60.6 us (0.948)
  other arithmetic: 4.74 us -> 2.42 us
  local copies, waits for them, and re-layouts: 7.57 us -> 6.64 us
    concatenate x1 -> x0, other arithmetic: 1.71 us -> none  [shards(): jnp.concatenate([w_query, key_value_weight.reshape(key_value_weight.shape...]
    unnamed x6 -> x3, local copies, waits for them, and re-layouts: 3.13 us -> 2.21 us
where the time goes in v9:
time: 60.6 us; the launch traced here: 60.4 us
  Pallas kernels  51.2 us (84%)
  local copies, waits for them, and re-layouts  6.64 us (11%)
  other arithmetic  2.42 us (4%)
    pallas_call x1, Pallas kernels, layer(): pl.pallas_call(layer_kernel, out_shape=jax.ShapeDtypeStruct((owned, width...  51.2 us
    unnamed x3, local copies, waits for them, and re-layouts  2.21 us

profile of v9, /device:TPU:1, one launch (start us, length us, event | category | flops | bytes accessed | tf_op | source)
XLA Modules:
  0.0 60.4 jit_solution(7593743289235586180)
XLA Ops:
  0.0 0.0 copy-start
  0.0 0.9 %copy-done = s32[64,8,32]{0,2,1:T(8,128)S(1)} copy-done((s32[64,8,32]{0,2,1:T(8,128)S(1)}, s32[64,8,32]{0,2,1:T(8,128)}, u32[]{:S(2)}) %copy-start) | copy-done | bytes 65560
  0.9 0.1 and.61
  1.1 0.5 broadcast.258
  1.6 0.7 %reduce.9 = s32[64]{0:T(128)S(1)} reduce(s32[64,1]{0,1:T(1,128)S(1)} %get-tuple-element.8, s32[]{:T(128)} %broadcast.258), dimensions={1}, to_apply=%slice_divide_fusion.reduce_sub_computation | reduce | bytes 516 | tf_op jit(solution)/shard_map/jit(floor_divide)/div | solution.py:439
  2.2 0.1 div.42
  2.4 0.1 broadcast_compare_fusion
  2.5 0.1 pad_convert_fusion
  2.6 1.1 %reshape.243.order_ref = bf16[128,128]{1,0:T(8,128)(2,1)} reshape(bf16[16,8,16,8]{3,2,1,0:T(8,128)(2,1)S(1)} %pad_convert_fusion) | data formatting | bytes 65536 | tf_op jit(solution)/shard_map/convert_element_type | solution.py:445
  3.8 0.7 %dynamic-slice_bitcast_fusion.1 = s32[64]{0:T(128)S(1)} fusion(s32[64,8]{0,1:T(8,128)} %param.20, s32[]{:T(128)S(6)} %select_n.57), kind=kLoop, calls=%fused_computation.40 | loop fusion | bytes 516 | tf_op jit(solution)/shard_map/jit(_where)/broadcast_in_dim | solution.py:452
  4.5 0.1 select_reduce_fusion.2
  4.6 0.1 multiply_cosine_fusion
  4.7 0.6 pad_maximum_fusion.trig_ref
  5.3 0.1 select_reduce_fusion.1
  5.5 0.1 fusion
  5.6 0.1 and.67
  5.7 0.1 and.68
  5.8 0.1 select_reduce_fusion
  5.9 0.1 broadcast_reduce_fusion
  6.0 0.1 add.85
  6.1 0.1 add.87
  6.2 0.1 compare_and_fusion
  6.3 0.7 %convert_element_type.32.mask_ref = s32[16,2816]{1,0:T(8,128)} reshape(s32[4,4,2816]{2,1,0:T(4,128)S(1)} %tile.2) | data formatting | bytes 360448 | tf_op jit(solution)/shard_map/convert_element_type | solution.py:471
  7.1 0.1 broadcast_compare_fusion.1
  7.2 0.7 %copy.15.unperm_ref = bf16[64,128]{1,0:T(8,128)(2,1)} copy(bf16[64,128]{0,1:T(8,128)(2,1)S(1)} %fusion.1) | data formatting | bytes 32768 | tf_op jit(solution)/shard_map/convert_element_type | solution.py:448
  7.9 51.2 %shard_map.109 = bf16[2,2048]{1,0:T(2,128)(2,1)} custom-call(bf16[4,2048]{1,0:T(4,128)(2,1)} %bitcast.22, f32[4,2048]{1,0:T(4,128)} %gains_ref.1, f32[2,256]{1,0:T(2,128)} %qkg_ref.1, bf16[128,128]{1,0:T(8,128)(2,1)} %reshape.243.order_ref, bf16[128,1024]{1,0:T(8,128)(2,1)} %wq_ref.1, bf16[128,2,256]{2,1,0:T(2,128)(2,1)} %kvw_ref.1, ...), custom_call_target="tpu_custom_call" | custom-call | tf_op jit(solution)/shard_map/pallas_call | solution.py:339
  59.1 1.3 %copy.17 = bf16[2,1,2048]{2,0,1:T(2,128)(2,1)} copy(bf16[2,1,2048]{2,0,1:T(2,128)(2,1)} %bitcast.21) | data formatting | bytes 16384
  (13 shorter events, 0.2 us)
Async XLA Ops:
  0.0 0.9 %copy-start = (s32[64,8,32]{0,2,1:T(8,128)S(1)}, s32[64,8,32]{0,2,1:T(8,128)}, u32[]{:S(2)}) copy-start(s32[64,8,32]{0,2,1:T(8,128)} %param.21) | copy-start | bytes 196612
